TPU v7x, 32 devices: a whole 2x2x4 slice. The times are simulated.
32 devices in a mesh: blk: 16 (over z, y, core), tp: 2 (over x).
Axes of the slice: x: 2, y: 2, z: 4, core: 2. Of those that a mesh axis runs over, the one named last changes fastest.
Arguments:
- frames: bfloat16 [4096, 1024], P('blk'), may hold values from -6 to 6
- clip_lengths: int32 [8], replicated, may hold values from 1 to 3841, 4096 in all
- text_states: bfloat16 [128, 1024], replicated, may hold values from -6 to 6
- text_segments: int32 [128], replicated, may hold values from 0 to 7, never falling along the last dimension, each value on 1 to 32 neighbouring positions
- gain_one: float32 [1024], replicated, may hold values from 0.1 to 1.9
- shift_one: float32 [1024], replicated, may hold values from -1.5 to 1.5
- gain_two: float32 [1024], replicated, may hold values from 0.1 to 1.9
- shift_two: float32 [1024], replicated, may hold values from -1.5 to 1.5
- gain_three: float32 [1024], replicated, may hold values from 0.1 to 1.9
- shift_three: float32 [1024], replicated, may hold values from -1.5 to 1.5
- query_weight: bfloat16 [1024, 1024], P(None, 'tp'), may hold values from -0.1875 to 0.1875
- key_weight: bfloat16 [1024, 1024], P(None, 'tp'), may hold values from -0.1875 to 0.1875
- value_weight: bfloat16 [1024, 1024], P(None, 'tp'), may hold values from -0.1875 to 0.1875
- output_weight: bfloat16 [1024, 1024], P('tp'), may hold values from -0.75 to 0.75
- cross_query: bfloat16 [1024, 1024], P(None, 'tp'), may hold values from -0.1875 to 0.1875
- cross_key: bfloat16 [1024, 1024], P(None, 'tp'), may hold values from -0.1875 to 0.1875
- cross_value: bfloat16 [1024, 1024], P(None, 'tp'), may hold values from -0.1875 to 0.1875
- cross_output: bfloat16 [1024, 1024], P('tp'), may hold values from -0.375 to 0.375
- inner_weight: bfloat16 [1024, 4096], P(None, 'tp'), may hold values from -0.1875 to 0.1875
- outer_weight: bfloat16 [4096, 1024], P('tp'), may hold values from -0.09375 to 0.09375
- cotangent: bfloat16 [4096, 1024], P('blk'), may hold values from -6 to 6
Outputs:
- result: bfloat16 [4096, 1024], P('blk')
- grad_frames: bfloat16 [4096, 1024], P('blk')
- grad_text: float32 [128, 1024], replicated
- grad_gain_one: float32 [1024], replicated
- grad_shift_one: float32 [1024], replicated
- grad_gain_two: float32 [1024], replicated
- grad_shift_two: float32 [1024], replicated
- grad_gain_three: float32 [1024], replicated
- grad_shift_three: float32 [1024], replicated
- grad_query_weight: float32 [1024, 1024], P(None, 'tp')
- grad_key_weight: float32 [1024, 1024], P(None, 'tp')
- grad_value_weight: float32 [1024, 1024], P(None, 'tp')
- grad_output_weight: float32 [1024, 1024], P('tp')
- grad_cross_query: float32 [1024, 1024], P(None, 'tp')
- grad_cross_key: float32 [1024, 1024], P(None, 'tp')
- grad_cross_value: float32 [1024, 1024], P(None, 'tp')
- grad_cross_output: float32 [1024, 1024], P('tp')
- grad_inner_weight: float32 [1024, 4096], P(None, 'tp')
- grad_outer_weight: float32 [4096, 1024], P('tp')
Inputs may be any that keep to these rules, and one draw needn't show every extreme that they name: `clip_lengths`: clips follow one another in the pack; one of them has 3841 frames. `text_segments`: text tokens of a clip stand together and in clip order; every clip has 1 to 32 of them, one exactly 32.
All inputs are finite; a program needn't handle non-finite values.
Results may differ from a plain program's by a relative error of at most 0.028.
Values may be sent and summed in bfloat16 or wider, within the bound.
No kernel may reach another device: no remote copies, remote signals or barrier semaphores. Data moves between devices by JAX's collectives and lax.ppermute only.
A program may use at most 384 MiB of HBM per device.

v0:
```python
import functools
import math
import jax
import jax.numpy as jnp
from jax import lax
from jax.experimental import pallas as pl
from jax.experimental.pallas import tpu as pltpu
from jax.sharding import PartitionSpec as P

HEAD_DIM = 64
NEGATIVE = -1e30
LARGE = 1 << 16
BF, F32 = jnp.bfloat16, jnp.float32


def lasting(microseconds):
    return pl.CostEstimate(flops=0, bytes_accessed=int(microseconds * 3.7e6), transcendentals=0)


def kernel_call(body, *, out_shape, least=LARGE, least_out=None, **options):
    many = isinstance(out_shape, (list, tuple))
    outs = [
        pltpu.HBM(o.shape, o.dtype) if math.prod(o.shape) >= (least_out or least) else o
        for o in (out_shape if many else [out_shape])
    ]
    call = pl.pallas_call(body, out_shape=outs if many else outs[0], **options)

    def run(*args):
        return call(
            *[
                pltpu.with_memory_space_constraint(a, pltpu.HBM) if a.size >= least else a
                for a in args
            ]
        )

    return run


def dg(left, right, dims):
    return lax.dot_general(left, right, (dims, ((), ())), preferred_element_type=F32)


def tile_ranges(positions, first, tile, chunk):
    rows = positions.reshape(-1, tile)
    starts = first.reshape(-1, tile)
    low = jnp.min(starts, axis=1) // chunk
    high = jnp.max(rows, axis=1) // chunk + 1
    clear = jnp.clip((jnp.max(starts, axis=1) + chunk - 1) // chunk, low, high)
    stop = jnp.clip((jnp.min(rows, axis=1) + 1) // chunk, clear, high)
    return jnp.stack([low, clear, stop, high], axis=1)


def allowed_keys(base, flip, chunk, rows, first):
    keys = (base + lax.broadcasted_iota(jnp.int32, (chunk, rows.shape[1]), 0)) ^ flip
    return (keys <= rows) & (keys >= first)


def attend_kernel(ranges, flips, q_ref, k_ref, v_ref, row_ref, first_ref, out_ref, log_ref, k_rows, chunk):
    tile = pl.program_id(0)
    total = k_ref.shape[1]

    @pl.when(tile == 0)
    def _():
        for base in range(0, total, chunk):
            k_rows[base : base + chunk, :] = k_ref[:, base : base + chunk].T

    queries = q_ref[...]
    rows, first = row_ref[...], first_ref[...]
    width = queries.shape[1]

    def work(masked):
        def step(index, carry):
            best, total_weight, acc = carry
            base = pl.multiple_of(index * chunk, chunk)
            score = jnp.dot(k_rows[pl.ds(base, chunk), :], queries, preferred_element_type=F32)
            if masked:
                allowed = allowed_keys(base, flips[0], chunk, rows, first)
                score = jnp.where(allowed, score, NEGATIVE)
            new_best = jnp.maximum(best, jnp.max(score, axis=0, keepdims=True))
            expo = jnp.exp(score - new_best)
            if masked:
                expo = jnp.where(allowed, expo, 0.0)
            fade = jnp.exp(best - new_best)
            total_weight = total_weight * fade + jnp.sum(expo, axis=0, keepdims=True)
            acc = acc * fade + jnp.dot(
                v_ref[:, pl.ds(base, chunk)], expo.astype(BF), preferred_element_type=F32
            )
            return new_best, total_weight, acc

        return step

    carry = (
        jnp.full((1, width), NEGATIVE, F32),
        jnp.zeros((1, width), F32),
        jnp.zeros((HEAD_DIM, width), F32),
    )
    carry = lax.fori_loop(ranges[tile, 0], ranges[tile, 1], work(True), carry)
    carry = lax.fori_loop(ranges[tile, 1], ranges[tile, 2], work(False), carry)
    best, total_weight, acc = lax.fori_loop(ranges[tile, 2], ranges[tile, 3], work(True), carry)
    out_ref[...] = acc / total_weight
    log_ref[...] = best + jnp.log(total_weight)


def attend(queries, keys, values, rows, first, flip, tile=512, chunk=1024):
    count, total = queries.shape[1], keys.shape[1]
    tile = min(tile, count)
    chunk = min(chunk, total)
    ranges = tile_ranges(rows, first, tile, chunk)
    whole = lambda i, r, f: (0, 0)
    part = lambda i, r, f: (0, i)
    return kernel_call(
        functools.partial(attend_kernel, chunk=chunk),
        grid_spec=pltpu.PrefetchScalarGridSpec(
            num_scalar_prefetch=2,
            grid=(count // tile,),
            in_specs=[
                pl.BlockSpec((HEAD_DIM, tile), part),
                pl.BlockSpec((HEAD_DIM, total), whole),
                pl.BlockSpec((HEAD_DIM, total), whole),
                pl.BlockSpec((1, tile), part),
                pl.BlockSpec((1, tile), part),
            ],
            out_specs=[pl.BlockSpec((HEAD_DIM, tile), part), pl.BlockSpec((1, tile), part)],
            scratch_shapes=[pltpu.VMEM((total, HEAD_DIM), BF)],
        ),
        out_shape=[
            jax.ShapeDtypeStruct((HEAD_DIM, count), F32),
            jax.ShapeDtypeStruct((1, count), F32),
        ],
        compiler_params=pltpu.CompilerParams(vmem_limit_bytes=(16 if total <= 4096 else 48) << 20),
        cost_estimate=lasting(15),
        least=1 << 30,
        name="attend",
    )(ranges, flip.reshape(1), queries, keys, values, rows.reshape(1, -1), first.reshape(1, -1))


def attend_back_kernel(
    ranges, flips, q_ref, k_ref, v_ref, row_ref, first_ref, out_ref, log_ref, do_ref,
    dq_ref, parts_ref, k_rows, v_rows, dk_ref, dv_ref, chunk,
):
    tile = pl.program_id(0)
    total = k_ref.shape[1]
    copies, blocks, _, _, sub = parts_ref.shape

    @pl.when(tile == 0)
    def _():
        for base in range(0, total, chunk):
            k_rows[base : base + chunk, :] = k_ref[:, base : base + chunk].T
            v_rows[base : base + chunk, :] = v_ref[:, base : base + chunk].T
        dk_ref[...] = jnp.zeros_like(dk_ref)
        dv_ref[...] = jnp.zeros_like(dv_ref)

    queries, grads = q_ref[...], do_ref[...]
    rows, first = row_ref[...], first_ref[...]
    log_total = log_ref[...]
    delta = jnp.sum(grads.astype(F32) * out_ref[...], axis=0, keepdims=True)

    def work(masked):
        def step(index, acc):
            base = pl.multiple_of(index * chunk, chunk)
            span = pl.ds(base, chunk)
            score = jnp.dot(k_rows[span, :], queries, preferred_element_type=F32)
            weights = jnp.exp(score - log_total)
            if masked:
                allowed = allowed_keys(base, flips[0], chunk, rows, first)
                weights = jnp.where(allowed, weights, 0.0)
            grad_weights = jnp.dot(v_rows[span, :], grads, preferred_element_type=F32)
            grad_score = (weights * (grad_weights - delta)).astype(BF)
            dv_ref[:, span] += dg(grads, weights.astype(BF), ((1,), (1,)))
            dk_ref[:, span] += dg(queries, grad_score, ((1,), (1,)))
            return acc + jnp.dot(k_ref[:, span], grad_score, preferred_element_type=F32)

        return step

    acc = jnp.zeros(queries.shape, F32)
    acc = lax.fori_loop(ranges[tile, 0], ranges[tile, 1], work(True), acc)
    acc = lax.fori_loop(ranges[tile, 1], ranges[tile, 2], work(False), acc)
    dq = lax.fori_loop(ranges[tile, 2], ranges[tile, 3], work(True), acc).astype(BF)
    for block in range(dq_ref.shape[0]):
        dq_ref[block] = dq[:, block * sub : (block + 1) * sub]

    @pl.when(tile == pl.num_programs(0) - 1)
    def _():
        for block in range(blocks):
            for copy in range(copies):
                at = (block * copies + copy) * sub
                parts_ref[copy, block, 0] = dk_ref[:, at : at + sub].astype(BF)
                parts_ref[copy, block, 1] = dv_ref[:, at : at + sub].astype(BF)


def attend_back(queries, keys, values, rows, first, flip, out, log_total, grads, sub, tile=512, chunk=1024):
    count, total = queries.shape[1], keys.shape[1]
    blocks, copies = count // sub, total // count
    tile = min(tile, count)
    chunk = min(chunk, total)
    ranges = tile_ranges(rows, first, tile, chunk)
    whole = lambda i, r, f: (0, 0)
    part = lambda i, r, f: (0, i)
    return kernel_call(
        functools.partial(attend_back_kernel, chunk=chunk),
        grid_spec=pltpu.PrefetchScalarGridSpec(
            num_scalar_prefetch=2,
            grid=(count // tile,),
            in_specs=[
                pl.BlockSpec((HEAD_DIM, tile), part),
                pl.BlockSpec((HEAD_DIM, total), whole),
                pl.BlockSpec((HEAD_DIM, total), whole),
                pl.BlockSpec((1, tile), part),
                pl.BlockSpec((1, tile), part),
                pl.BlockSpec((HEAD_DIM, tile), part),
                pl.BlockSpec((1, tile), part),
                pl.BlockSpec((HEAD_DIM, tile), part),
            ],
            out_specs=[
                pl.BlockSpec((tile // sub, HEAD_DIM, sub), lambda i, r, f: (i, 0, 0)),
                pl.BlockSpec((copies, blocks, 2, HEAD_DIM, sub), lambda i, r, f: (0, 0, 0, 0, 0)),
            ],
            scratch_shapes=[
                pltpu.VMEM((total, HEAD_DIM), BF),
                pltpu.VMEM((total, HEAD_DIM), BF),
                pltpu.VMEM((HEAD_DIM, total), F32),
                pltpu.VMEM((HEAD_DIM, total), F32),
            ],
        ),
        out_shape=[
            jax.ShapeDtypeStruct((blocks, HEAD_DIM, sub), BF),
            jax.ShapeDtypeStruct((copies, blocks, 2, HEAD_DIM, sub), BF),
        ],
        compiler_params=pltpu.CompilerParams(vmem_limit_bytes=(24 if total <= 4096 else 60) << 20),
        cost_estimate=lasting(17),
        least=1 << 30,
        name="attend_back",
    )(ranges, flip.reshape(1), queries, keys, values, rows.reshape(1, -1), first.reshape(1, -1), out, log_total, grads)


EPSILON = 1e-05
SWAP = [(0, 1), (1, 0)]


def after(values, token):
    return lax.optimization_barrier((values, token))[0]


def over_x(value):
    return lax.ppermute(value, "tp", SWAP)


def over_blk(value, bit):
    return lax.ppermute(value, "blk", [(i, i ^ bit) for i in range(lax.axis_size("blk"))])


def normalize(values):
    centre = values - jnp.mean(values, axis=-1, keepdims=True)
    spread = lax.rsqrt(jnp.mean(centre * centre, axis=-1, keepdims=True) + EPSILON)
    return centre * spread, spread


def norm_back(values, gain, grad):
    hat, spread = normalize(values)
    scaled = grad * gain
    through = spread * (
        scaled
        - jnp.mean(scaled, axis=-1, keepdims=True)
        - hat * jnp.mean(scaled * hat, axis=-1, keepdims=True)
    )
    return through, jnp.sum(grad * hat, axis=0), jnp.sum(grad, axis=0)


def clip_rows(positions, clip_lengths):
    index = jnp.arange(clip_lengths.shape[0], dtype=jnp.int32)
    starts = jnp.sum(jnp.where(index[None, :] < index[:, None], clip_lengths[None, :], 0), axis=1)
    ends = starts + clip_lengths
    segment = jnp.sum((positions[:, None] >= ends[None, :]).astype(jnp.int32), axis=1)
    match = segment[:, None] == index[None, :]
    first = jnp.sum(jnp.where(match, starts[None, :], 0), axis=1)
    return segment, first


def matmul(left, right):
    return jnp.dot(left, right, preferred_element_type=F32)


def matmul_nt(left, right):
    return dg(left, right, ((1,), (1,)))


def matmul_tn(left, right):
    return dg(left, right, ((0,), (0,)))


def first_hop(weight, core):
    return over_x(halves(weight, core))


def weld_kernel(core, *refs):
    count = len(refs) // 3
    for which in range(count):
        first, second, out = refs[which], refs[count + which], refs[2 * count + which]
        chosen = pl.program_id(0) == core[0]

        @pl.when(chosen)
        def _():
            out[...] = first[...]

        @pl.when(jnp.logical_not(chosen))
        def _():
            out[...] = second[...]


def weld(own, other, core):
    outs = [jax.ShapeDtypeStruct((2 * a.shape[0], a.shape[1]), a.dtype) for a in own]
    return kernel_call(
        weld_kernel,
        grid_spec=pltpu.PrefetchScalarGridSpec(
            num_scalar_prefetch=1,
            grid=(2,),
            in_specs=[whole_spec(a) for a in list(own) + list(other)],
            out_specs=[pl.BlockSpec(a.shape, lambda i, c: (i, 0)) for a in own],
        ),
        out_shape=outs,
        compiler_params=pltpu.CompilerParams(vmem_limit_bytes=24 << 20),
        cost_estimate=lasting(4),
        name="weld",
    )(core.reshape(1), *own, *other)


def in_order(own, other, tp):
    return jnp.concatenate([jnp.where(tp == 0, own, other), jnp.where(tp == 0, other, own)])


def whole_spec(array):
    shape = array.shape
    return pl.BlockSpec(shape, lambda *_: (0,) * len(shape))


def norm_rows(values):
    centre = values - jnp.mean(values, axis=-1, keepdims=True)
    spread = lax.rsqrt(jnp.mean(centre * centre, axis=-1, keepdims=True) + EPSILON)
    return centre * spread, spread


def norm_rows_back(values, gain, grad):
    hat, spread = norm_rows(values)
    scaled = grad * gain
    through = spread * (
        scaled
        - jnp.mean(scaled, axis=-1, keepdims=True)
        - hat * jnp.mean(scaled * hat, axis=-1, keepdims=True)
    )
    return through, jnp.sum(grad * hat, axis=0, keepdims=True), jnp.sum(grad, axis=0, keepdims=True)


def text_weights(keys, queries, allowed):
    score = dg(keys, queries, ((0,), (0,)))
    score = jnp.where(allowed, score, NEGATIVE)
    expo = jnp.exp(score - jnp.max(score, axis=0, keepdims=True))
    expo = jnp.where(allowed, expo, 0.0)
    return expo / jnp.sum(expo, axis=0, keepdims=True)


def embed_kernel(x_ref, gain, shift, wq_ref, wk_ref, wv_ref, rows_ref, out_ref, scale):
    hat, _ = norm_rows(x_ref[...].astype(F32))
    rows = (hat * gain[...] + shift[...]).astype(BF)
    rows_ref[...] = rows
    blocks, _, _, sub = out_ref.shape
    copies = rows.shape[0] // sub
    for which, weight in enumerate([wq_ref, wk_ref, wv_ref]):
        value = jnp.dot(rows, weight[...], preferred_element_type=F32)
        value = (value * scale if which == 0 else value).astype(BF).T
        for block in range(blocks):
            head, copy = divmod(block, copies)
            out_ref[block, which] = value[
                head * HEAD_DIM : (head + 1) * HEAD_DIM, copy * sub : (copy + 1) * sub
            ]


def embed(frames, gain, shift, weights, blocks, sub, scale):
    args = [frames, gain, shift, *weights]
    outs = [
        jax.ShapeDtypeStruct(frames.shape, BF),
        jax.ShapeDtypeStruct((blocks, 3, HEAD_DIM, sub), BF),
    ]
    return kernel_call(
        functools.partial(embed_kernel, scale=scale),
        grid=(1,),
        in_specs=[whole_spec(a) for a in args],
        out_specs=[whole_spec(o) for o in outs],
        out_shape=outs,
        compiler_params=pltpu.CompilerParams(vmem_limit_bytes=24 << 20),
        cost_estimate=lasting(5),
        least=1 << 30,
        name="embed",
    )(*args)


def cross_kernel(
    a_own, a_other, x_ref, gain_two, shift_two, gain_three, shift_three, wo_own, wo_other,
    wq_own, wq_other, wc_own, wc_other, tk_ref, tv_ref, segment, text_segment,
    x1_ref, x2_ref, h2_ref, h3_ref, q_ref, oc_ref, c_own, c_other, scale,
):
    width = a_own.shape[0]
    change = jnp.dot(a_own[...].T, wo_own[...], preferred_element_type=F32)
    change += jnp.dot(a_other[...].T, wo_other[...], preferred_element_type=F32)
    x1 = x_ref[...].astype(F32) + change
    x1_ref[...] = x1
    hat, _ = norm_rows(x1)
    h2 = (hat * gain_two[...] + shift_two[...]).astype(BF)
    h2_ref[...] = h2
    allowed = text_segment[...] == segment[...]
    crosses = []
    for side, wq in enumerate([wq_own, wq_other]):
        qc = (jnp.dot(h2, wq[...], preferred_element_type=F32) * scale).astype(BF)
        q_t = qc.T
        q_ref[side] = q_t
        parts = []
        for head in range(width // HEAD_DIM):
            span = slice(head * HEAD_DIM, (head + 1) * HEAD_DIM)
            weights = text_weights(tk_ref[side, span, :], q_t[span, :], allowed)
            parts.append(
                jnp.dot(tv_ref[side, span, :], weights.astype(BF), preferred_element_type=F32)
            )
        oc = jnp.concatenate(parts, axis=0)
        oc_ref[side] = oc
        crossed = oc.astype(BF)
        (c_own if side == 0 else c_other)[...] = crossed
        crosses.append(crossed.T)
    change = jnp.dot(crosses[0], wc_own[...], preferred_element_type=F32)
    change += jnp.dot(crosses[1], wc_other[...], preferred_element_type=F32)
    x2 = x1 + change
    x2_ref[...] = x2
    hat, _ = norm_rows(x2)
    h3_ref[...] = (hat * gain_three[...] + shift_three[...]).astype(BF)


def cross_forward(a_both, x_own, norms, output_both, query_both, cross_both, tk, tv, segment, text_segment, scale):
    half, depth = x_own.shape
    width = a_both[0].shape[0]
    args = [*a_both, x_own, *norms, *output_both, *query_both, *cross_both, tk, tv, segment, text_segment]
    shape = jax.ShapeDtypeStruct
    outs = [
        shape((half, depth), F32), shape((half, depth), F32), shape((half, depth), BF),
        shape((half, depth), BF), shape((2, width, half), BF), shape((2, width, half), F32),
        shape((width, half), BF), shape((width, half), BF),
    ]
    return kernel_call(
        functools.partial(cross_kernel, scale=scale),
        grid=(1,),
        in_specs=[whole_spec(a) for a in args],
        out_specs=[whole_spec(o) for o in outs],
        out_shape=outs,
        compiler_params=pltpu.CompilerParams(vmem_limit_bytes=28 << 20),
        cost_estimate=lasting(7),
        name="cross_forward",
    )(*args)


def cross_back_kernel(
    dh_own, dh_got, dy_ref, x1_ref, x2_ref, gain_two, gain_three, wo_own, wo_other,
    wq_own, wq_other, wc_own, wc_other, tk_ref, tv_ref, q_ref, oc_ref, segment, text_segment,
    dx1_ref, dx1_low_ref, dx2_low_ref, dq_own, dq_other, da_own, da_other, text_own, text_other,
    small_ref, scale,
):
    width = tk_ref.shape[1]
    dh3 = dh_own[...].astype(F32) + dh_got[...].astype(F32)
    through, gain_grad, shift_grad = norm_rows_back(x2_ref[...], gain_three[...], dh3)
    small_ref[2:3, :] = gain_grad
    small_ref[3:4, :] = shift_grad
    dx2 = dy_ref[...].astype(F32) + through
    low = dx2.astype(BF)
    dx2_low_ref[...] = low
    allowed = text_segment[...] == segment[...]
    dqs = []
    for side, wc in enumerate([wc_own, wc_other]):
        dc_t = dg(low, wc[...], ((1,), (1,))).astype(BF).T
        parts = []
        for head in range(width // HEAD_DIM):
            span = slice(head * HEAD_DIM, (head + 1) * HEAD_DIM)
            queries, grads = q_ref[side, span, :], dc_t[span, :]
            weights = text_weights(tk_ref[side, span, :], queries, allowed)
            delta = jnp.sum(grads.astype(F32) * oc_ref[side, span, :], axis=0, keepdims=True)
            grad_weights = dg(tv_ref[side, span, :], grads, ((0,), (0,)))
            grad_score = (weights * (grad_weights - delta)).astype(BF)
            dq = jnp.dot(tk_ref[side, span, :], grad_score, preferred_element_type=F32).astype(BF)
            parts.append(dq * jnp.asarray(scale, BF))
            text_ref = text_own if side == 0 else text_other
            text_ref[0, span, :] = dg(queries, grad_score, ((1,), (1,))).astype(text_ref.dtype)
            text_ref[1, span, :] = dg(grads, weights.astype(BF), ((1,), (1,))).astype(text_ref.dtype)
        dq = jnp.concatenate(parts, axis=0)
        (dq_own if side == 0 else dq_other)[...] = dq
        dqs.append(dq.T)
    dh2 = dg(dqs[0], wq_own[...], ((1,), (1,))) + dg(dqs[1], wq_other[...], ((1,), (1,)))
    through, gain_grad, shift_grad = norm_rows_back(x1_ref[...], gain_two[...], dh2)
    small_ref[0:1, :] = gain_grad
    small_ref[1:2, :] = shift_grad
    dx1 = dx2 + through
    dx1_ref[...] = dx1
    low = dx1.astype(BF)
    dx1_low_ref[...] = low
    for ref, wo in [(da_own, wo_own), (da_other, wo_other)]:
        ref[...] = dg(low, wo[...], ((1,), (1,))).astype(BF).T


def cross_backward(
    dh_own, dh_got, dy_own, x1, x2, gain_two, gain_three, output_both, query_both, cross_both,
    tk, tv, q_t, oc, segment, text_segment, scale,
):
    half, depth = x1.shape
    width, text = tk.shape[1], tk.shape[2]
    args = [
        dh_own, dh_got, dy_own, x1, x2, gain_two, gain_three, *output_both, *query_both,
        *cross_both, tk, tv, q_t, oc, segment, text_segment,
    ]
    shape = jax.ShapeDtypeStruct
    outs = [
        shape((half, depth), F32), shape((half, depth), BF), shape((half, depth), BF),
        *[shape((width, half), BF)] * 4, shape((2, width, text), F32), shape((2, width, text), BF),
        shape((4, depth), F32),
    ]
    return kernel_call(
        functools.partial(cross_back_kernel, scale=scale),
        grid=(1,),
        in_specs=[whole_spec(a) for a in args],
        out_specs=[whole_spec(o) for o in outs],
        out_shape=outs,
        compiler_params=pltpu.CompilerParams(vmem_limit_bytes=28 << 20),
        cost_estimate=lasting(9),
        name="cross_backward",
    )(*args)


def hidden_kernel(tp_ref, h_own, h_other, dy_ref, wi_ref, wo_ref, g_ref, du_ref, own_ref, other_ref, acc):
    step, half = pl.program_id(0), h_own.shape[0]
    tp = tp_ref[0]

    @pl.when(step == 0)
    def _():
        acc[...] = jnp.zeros_like(acc)

    for part, h_ref in enumerate([h_own, h_other]):
        rows = slice(part * half, (part + 1) * half)
        base = jnp.where(tp == part, 0, half)
        dy = dy_ref[pl.ds(pl.multiple_of(base, half), half), :]
        pre = jnp.dot(h_ref[...], wi_ref[...], preferred_element_type=F32)
        cdf = 0.5 * (1.0 + lax.erf(pre * (0.5**0.5)))
        density = jnp.exp(-0.5 * pre * pre) * 0.3989422804014327
        g_ref[rows, :] = (pre * cdf).astype(BF)
        grad = dg(dy, wo_ref[...], ((1,), (1,)))
        grad = (grad * (cdf + pre * density)).astype(BF)
        du_ref[rows, :] = grad
        acc[rows, :] += dg(grad, wi_ref[...], ((1,), (1,)))

    @pl.when(step == pl.num_programs(0) - 1)
    def _():
        own_ref[...] = acc[:half, :]
        other_ref[...] = acc[half:, :].astype(BF)


def hidden_pass(h_own, h_other, cotangent, inner, outer, tp, tile=512):
    half, depth = h_own.shape
    units = inner.shape[1]
    shape = jax.ShapeDtypeStruct
    return kernel_call(
        hidden_kernel,
        grid_spec=pltpu.PrefetchScalarGridSpec(
            num_scalar_prefetch=1,
            grid=(units // tile,),
            in_specs=[
                whole_spec(h_own), whole_spec(h_other), whole_spec(cotangent),
                pl.BlockSpec((depth, tile), lambda i, t: (0, i)),
                pl.BlockSpec((tile, depth), lambda i, t: (i, 0)),
            ],
            out_specs=[
                pl.BlockSpec((2 * half, tile), lambda i, t: (0, i)),
                pl.BlockSpec((2 * half, tile), lambda i, t: (0, i)),
                pl.BlockSpec((half, depth), lambda i, t: (0, 0)),
                pl.BlockSpec((half, depth), lambda i, t: (0, 0)),
            ],
            scratch_shapes=[pltpu.VMEM((2 * half, depth), F32)],
        ),
        out_shape=[
            shape((2 * half, units), BF), shape((2 * half, units), BF),
            shape((half, depth), F32), shape((half, depth), BF),
        ],
        compiler_params=pltpu.CompilerParams(vmem_limit_bytes=20 << 20),
        cost_estimate=lasting(10),
        least=1 << 30,
        name="hidden_pass",
    )(tp.reshape(1), h_own, h_other, cotangent, inner, outer)


def hidden_grads_kernel(
    place, h_own, h_other, dy_ref, g_ref, du_ref, wo_ref, both_ref, y_own, y_other, h_all, dy_all, acc
):
    step, half = pl.program_id(0), h_own.shape[0]
    tp = place[0]

    @pl.when(step == 0)
    def _():
        acc[...] = jnp.zeros_like(acc)
        h_all[:half, :] = h_own[...]
        h_all[half:, :] = h_other[...]
        for part in range(2):
            base = jnp.where(tp == part, 0, half)
            dy_all[part * half : (part + 1) * half, :] = dy_ref[
                pl.ds(pl.multiple_of(base, half), half), :
            ]

    acc[...] += jnp.dot(g_ref[...], wo_ref[...], preferred_element_type=F32)
    depth = h_own.shape[1]
    both_ref[:, :depth] = jnp.dot(g_ref[...].T, dy_all[...], preferred_element_type=F32).astype(BF)
    both_ref[:, depth:] = jnp.dot(du_ref[...].T, h_all[...], preferred_element_type=F32).astype(BF)

    @pl.when(step == pl.num_programs(0) - 1)
    def _():
        y_own[...] = acc[:half, :]
        y_other[...] = acc[half:, :].astype(BF)


def hidden_grads(h_own, h_other, cotangent, g, du, outer, tp, tile=256):
    half, depth = h_own.shape
    units = outer.shape[0]
    shape = jax.ShapeDtypeStruct
    across = lambda i, p: (0, i)
    down = lambda i, p: (i, 0)
    still = lambda i, p: (0, 0)
    return kernel_call(
        hidden_grads_kernel,
        grid_spec=pltpu.PrefetchScalarGridSpec(
            num_scalar_prefetch=1,
            grid=(units // tile,),
            in_specs=[
                whole_spec(h_own), whole_spec(h_other), whole_spec(cotangent),
                pl.BlockSpec((2 * half, tile), across), pl.BlockSpec((2 * half, tile), across),
                pl.BlockSpec((tile, depth), down),
            ],
            out_specs=[
                pl.BlockSpec((tile, 2 * depth), down),
                pl.BlockSpec((half, depth), still), pl.BlockSpec((half, depth), still),
            ],
            scratch_shapes=[
                pltpu.VMEM((2 * half, depth), BF),
                pltpu.VMEM((2 * half, depth), BF),
                pltpu.VMEM((2 * half, depth), F32),
            ],
        ),
        out_shape=[
            shape((units, 2 * depth), BF), shape((half, depth), F32), shape((half, depth), BF),
        ],
        compiler_params=pltpu.CompilerParams(vmem_limit_bytes=20 << 20),
        cost_estimate=lasting(9),
        least=1 << 30,
        least_out=LARGE,
        name="hidden_grads",
    )(tp.reshape(1), h_own, h_other, cotangent, g, du, outer)


def hidden_out_kernel(both_ref, outer_ref, inner_ref):
    depth = outer_ref.shape[1]
    outer_ref[...] = both_ref[:, :depth].astype(F32)
    inner_ref[...] = both_ref[:, depth:].astype(F32).T


def hidden_out(both, tile=256):
    units, depth = both.shape[0], both.shape[1] // 2
    return kernel_call(
        hidden_out_kernel,
        grid=(units // tile,),
        in_specs=[pl.BlockSpec((tile, 2 * depth), lambda i: (i, 0))],
        out_specs=[
            pl.BlockSpec((tile, depth), lambda i: (i, 0)), pl.BlockSpec((depth, tile), lambda i: (0, i))
        ],
        out_shape=[
            jax.ShapeDtypeStruct((units, depth), F32), jax.ShapeDtypeStruct((depth, units), F32)
        ],
        compiler_params=pltpu.CompilerParams(vmem_limit_bytes=16 << 20),
        cost_estimate=lasting(9),
        name="hidden_out",
    )(both)


def pair_grads_kernel(core, *refs):
    send, keep = refs[-2:]
    ins = refs[:-2]
    rows = send.shape[0]
    for which in range(len(ins) // 4):
        left_own, left_other, right_own, right_other = ins[4 * which : 4 * which + 4]
        depth = right_own.shape[1]
        for ref, side in [(send, 1 - core[0]), (keep, core[0])]:
            span = pl.ds(pl.multiple_of(side * rows, rows), rows)
            total = jnp.dot(left_own[span, :], right_own[...], preferred_element_type=F32)
            total += jnp.dot(left_other[span, :], right_other[...], preferred_element_type=F32)
            ref[:, which * depth : (which + 1) * depth] = total.astype(BF)


def pair_grads(groups, core):
    args = [array for group in groups for array in group]
    features, depth = groups[0][0].shape[0], groups[0][2].shape[1]
    columns = depth * len(groups)
    out = jax.ShapeDtypeStruct((features // 2, columns), BF)
    return kernel_call(
        pair_grads_kernel,
        grid_spec=pltpu.PrefetchScalarGridSpec(
            num_scalar_prefetch=1,
            grid=(1,),
            in_specs=[whole_spec(a) for a in args],
            out_specs=[whole_spec(out), whole_spec(out)],
        ),
        out_shape=[out, out],
        compiler_params=pltpu.CompilerParams(vmem_limit_bytes=24 << 20),
        cost_estimate=lasting(4),
        name="pair_grads",
    )(core.reshape(1), *args)


def fold_kernel(sides, *refs):
    count = len(refs) // 4
    ins, outs = refs[: 2 * count], refs[2 * count :]
    first = pl.program_id(0) < pl.num_programs(0) // 2
    for which in range(count):
        total = ins[2 * which][...].astype(F32) + ins[2 * which + 1][...].astype(F32)
        total = total.astype(BF)

        @pl.when(first)
        def _():
            outs[2 * which][...] = total

        @pl.when(jnp.logical_not(first))
        def _():
            outs[2 * which + 1][...] = total


def fold(pairs, sides):
    least = min(keep.shape[0] for keep, _ in pairs)
    if least % 16:
        sums = [(keep.astype(F32) + got.astype(F32)).astype(BF) for keep, got in pairs]
        return [(halves(t, 1 - side), halves(t, side)) for t, side in zip(sums, sides)]
    parts = 2 if least % 32 == 0 else 1
    args, in_specs, out_specs, outs = [], [], [], []
    for which, (keep, got) in enumerate(pairs):
        rows, columns = keep.shape
        block = rows // (2 * parts)
        place = lambda i, s, which=which: (
            jnp.where(i < parts, (1 - s[which]) * parts + i, s[which] * parts + i - parts), 0
        )
        args += [keep, got]
        in_specs += [pl.BlockSpec((block, columns), place)] * 2
        out_specs += [
            pl.BlockSpec((block, columns), lambda i, s: (jnp.minimum(i, parts - 1), 0)),
            pl.BlockSpec((block, columns), lambda i, s: (jnp.maximum(i - parts, 0), 0)),
        ]
        outs += [jax.ShapeDtypeStruct((rows // 2, columns), BF)] * 2
    got = kernel_call(
        fold_kernel,
        grid_spec=pltpu.PrefetchScalarGridSpec(
            num_scalar_prefetch=1,
            grid=(2 * parts,),
            in_specs=in_specs,
            out_specs=out_specs,
        ),
        out_shape=outs,
        compiler_params=pltpu.CompilerParams(vmem_limit_bytes=12 << 20),
        cost_estimate=lasting(3),
        name="fold",
    )(jnp.stack(sides), *args)
    return [(got[2 * i], got[2 * i + 1]) for i in range(len(pairs))]


def piece_places(count, order):
    places = []
    for device in range(count):
        index = 0
        for bit in order:
            index = index * 2 + (device // bit) % 2
        places.append(index)
    return places


def widen_kernel(devices, *refs, group, height):
    ins, outs = refs[: 2 * group], refs[2 * group :]
    columns = ins[0].shape[2]
    for slot in range(group):
        rows = ins[slot].shape[1]
        place = slice(slot * rows, (slot + 1) * rows)
        width = outs[0].shape[1]
        for which in range(3):
            outs[which][place, :] = ins[slot][0, :, which * width : (which + 1) * width].astype(F32)
    turned = []
    for slot in range(group):
        source = ins[group + slot]
        place = slice(slot * height, (slot + 1) * height)
        depth = outs[3].shape[1]
        at = 0
        for which in range(3):
            filled, found = 0, []
            while filled < depth:
                part, column = divmod(at, columns)
                count = min(columns - column, depth - filled)
                found.append(
                    source[0, part * height : (part + 1) * height, column : column + count]
                )
                if which < 2:
                    outs[3 + which][place, filled : filled + count] = found[-1].astype(F32)
                filled, at = filled + count, at + count
        turned.append(jnp.concatenate([value.astype(F32) for value in found], axis=1))
    outs[5][...] = jnp.concatenate(turned, axis=0).T


def widen(gathered, head_order, pair_order, rows, height, width, depth):
    count, total, columns = gathered.shape
    group = max(4, 128 // height)
    tables = []
    for order in (head_order, pair_order):
        places = piece_places(count, order)
        tables.append([places.index(place) for place in range(count)])
    spec = lambda kind, slot: pl.BlockSpec(
        (1, rows, columns), lambda j, t: (t[kind, j * group + slot], kind, 0)
    )
    shape = jax.ShapeDtypeStruct
    outs = [shape((count * rows, width), F32)] * 3 + [shape((count * height, depth), F32)] * 2
    outs += [shape((depth, count * height), F32)]
    down = lambda j, t: (j, 0)
    return kernel_call(
        functools.partial(widen_kernel, group=group, height=height),
        grid_spec=pltpu.PrefetchScalarGridSpec(
            num_scalar_prefetch=1,
            grid=(count // group,),
            in_specs=[spec(kind, slot) for kind in range(2) for slot in range(group)],
            out_specs=[pl.BlockSpec((group * rows, width), down)] * 3
            + [pl.BlockSpec((group * height, depth), down)] * 2
            + [pl.BlockSpec((depth, group * height), lambda j, t: (0, j))],
        ),
        out_shape=outs,
        compiler_params=pltpu.CompilerParams(vmem_limit_bytes=24 << 20),
        cost_estimate=lasting(7),
        name="widen",
    )(jnp.asarray(tables, jnp.int32), *[gathered] * (2 * group))


class Stream:
    def __init__(self, send, keep, order, blk):
        self.order, self.blk, self.phase, self.keep = order, blk, 0, keep
        self.got, self.sent = over_blk(send, order[0]), send

    def step(self):
        count, phase = len(self.order), self.phase
        if phase is None:
            return
        self.phase += 1
        if phase < count - 1:
            bit = self.order[phase + 1]
            ((send, self.keep),) = fold([(self.keep, self.got)], [(self.blk // bit) % 2])
            self.got, self.sent = over_blk(send, bit), send
        elif phase < 2 * count - 1:
            if phase == count - 1:
                piece = self.keep.astype(F32) + self.got.astype(F32)
                self.keep = piece.astype(BF)[None]
            else:
                self.keep = join(self.keep, self.got)
            self.got, self.sent = over_blk(self.keep, self.order[2 * count - 2 - phase]), self.keep
            if phase == 2 * count - 2:
                self.phase = None

    def piece(self):
        return (self.keep.astype(F32) + self.got.astype(F32)).astype(BF)

    def result(self, widths):
        return unpack(self.keep, self.got, self.order, widths)


def step_together(streams):
    bits = [stream.order[stream.phase + 1] for stream in streams]
    sides = [(stream.blk // bit) % 2 for stream, bit in zip(streams, bits)]
    halved = fold([(stream.keep, stream.got) for stream in streams], sides)
    for stream, (send, keep), bit in zip(streams, halved, bits):
        stream.phase += 1
        stream.keep, stream.sent, stream.got = keep, send, over_blk(send, bit)


def last_kernel(head_keep, head_got, pair_keep, pair_got, out_ref):
    rows, columns = head_keep.shape
    out_ref[:rows, :] = (head_keep[...].astype(F32) + head_got[...].astype(F32)).astype(BF)
    height = pair_keep.shape[0]
    pair = (pair_keep[...].astype(F32) + pair_got[...].astype(F32)).astype(BF)
    for part in range(pair.shape[1] // columns):
        at = rows + part * height
        out_ref[at : at + height, :] = pair[:, part * columns : (part + 1) * columns]


def last_halves(heads, pairs):
    args = [heads.keep, heads.got, pairs.keep, pairs.got]
    rows, columns = heads.keep.shape
    height = pairs.keep.shape[0] * (pairs.keep.shape[1] // columns)
    out = jax.ShapeDtypeStruct((rows + height, columns), BF)
    return kernel_call(
        last_kernel,
        grid=(1,),
        in_specs=[whole_spec(a) for a in args],
        out_specs=whole_spec(out),
        out_shape=out,
        cost_estimate=lasting(2),
        name="last_halves",
    )(*args)


class Butterfly:
    def __init__(self, value, order, wire):
        self.value, self.order, self.phase, self.wire = value, order, 0, wire
        self.got, self.sent = over_blk(value.astype(wire), order[0]), value

    def step(self):
        if self.phase is None:
            return
        self.value = self.value + self.got.astype(F32)
        self.phase += 1
        if self.phase < len(self.order):
            self.got = over_blk(self.value.astype(self.wire), self.order[self.phase])
            self.sent = self.value
        else:
            self.got, self.phase = jnp.zeros((), F32), None


def meet(streams, others):
    got, others = lax.optimization_barrier(([s.got for s in streams], others))
    for stream, value in zip(streams, got):
        stream.got = value
    return others


def project_back_kernel(tp, back_ref, *refs):
    weights, (own_ref, other_ref) = refs[:3], refs[3:]
    half = own_ref.shape[0]
    total = None
    for which, weight in enumerate(weights):
        part = dg(back_ref[which].T, weight[...], ((1,), (1,)))
        total = part if total is None else total + part
    first, second = total[:half, :], total[half:, :]
    own_ref[...] = jnp.where(tp[0] == 0, first, second)
    other_ref[...] = jnp.where(tp[0] == 0, second, first).astype(BF)


def project_back(back, weights, tp):
    rows, depth = back.shape[2], weights[0].shape[0]
    args = [back, *weights]
    outs = [
        jax.ShapeDtypeStruct((rows // 2, depth), F32), jax.ShapeDtypeStruct((rows // 2, depth), BF)
    ]
    return kernel_call(
        project_back_kernel,
        grid_spec=pltpu.PrefetchScalarGridSpec(
            num_scalar_prefetch=1,
            grid=(1,),
            in_specs=[whole_spec(a) for a in args],
            out_specs=[whole_spec(o) for o in outs],
        ),
        out_shape=outs,
        compiler_params=pltpu.CompilerParams(vmem_limit_bytes=16 << 20),
        cost_estimate=lasting(4),
        name="project_back",
    )(tp.reshape(1), *args)


def head_grads_kernel(core, back_ref, rows_ref, send, keep, turned):
    turned[...] = rows_ref[...].T
    rows, width = send.shape[0], back_ref.shape[1]
    for ref, side in [(send, 1 - core[0]), (keep, core[0])]:
        part = turned[pl.ds(pl.multiple_of(side * rows, rows), rows), :]
        for which in range(3):
            ref[:, which * width : (which + 1) * width] = dg(
                part, back_ref[which], ((1,), (1,))
            ).astype(BF)


def head_grads(back, normed, core):
    rows, depth = normed.shape
    out = jax.ShapeDtypeStruct((depth // 2, 3 * back.shape[1]), BF)
    return kernel_call(
        head_grads_kernel,
        grid_spec=pltpu.PrefetchScalarGridSpec(
            num_scalar_prefetch=1,
            grid=(1,),
            in_specs=[whole_spec(back), whole_spec(normed)],
            out_specs=[whole_spec(out), whole_spec(out)],
            scratch_shapes=[pltpu.VMEM((depth, rows), BF)],
        ),
        out_shape=[out, out],
        compiler_params=pltpu.CompilerParams(vmem_limit_bytes=16 << 20),
        cost_estimate=lasting(4),
        name="head_grads",
    )(core.reshape(1), back, normed)


def combine_kernel(dq_ref, parts_ref, got_ref, out_ref, scale):
    out_ref[:, 0] = dq_ref[...] * jnp.asarray(scale, BF)
    out_ref[:, 1:] = (parts_ref[0].astype(F32) + got_ref[...].astype(F32)).astype(BF)


def combine(dq, parts, got, scale):
    blocks, _, sub = dq.shape
    part = min(4, blocks)
    return kernel_call(
        functools.partial(combine_kernel, scale=scale),
        grid=(blocks // part,),
        in_specs=[
            pl.BlockSpec((part, HEAD_DIM, sub), lambda i: (i, 0, 0)),
            pl.BlockSpec((1, part, 2, HEAD_DIM, sub), lambda i: (0, i, 0, 0, 0)),
            pl.BlockSpec((part, 2, HEAD_DIM, sub), lambda i: (i, 0, 0, 0)),
        ],
        out_specs=pl.BlockSpec((part, 3, HEAD_DIM, sub), lambda i: (i, 0, 0, 0)),
        out_shape=jax.ShapeDtypeStruct((blocks, 3, HEAD_DIM, sub), BF),
        cost_estimate=lasting(3.5),
        name="combine",
    )(dq, parts, got)


def join_kernel(low_ref, high_ref, out_ref):
    for part, ref in enumerate([low_ref, high_ref]):

        @pl.when(pl.program_id(0) == part)
        def _():
            out_ref[...] = ref[...]


def join(low, high):
    shape = low.shape
    still = lambda i: (0,) * len(shape)
    return kernel_call(
        join_kernel,
        grid=(2,),
        in_specs=[pl.BlockSpec(shape, still)] * 2,
        out_specs=pl.BlockSpec(shape, lambda i: (i,) + (0,) * (len(shape) - 1)),
        out_shape=jax.ShapeDtypeStruct((2 * shape[0],) + shape[1:], low.dtype),
        compiler_params=pltpu.CompilerParams(vmem_limit_bytes=12 << 20),
        cost_estimate=lasting(2),
        name="join",
    )(low, high)


def halves(value, which):
    rows = value.shape[0] // 2
    return lax.dynamic_slice_in_dim(value, which * rows, rows, 0)


def piece_index(order):
    blk = lax.axis_index("blk")
    index = 0
    for bit in order:
        index = index * 2 + (blk // bit) % 2
    return index


def unpack_kernel(index, low_ref, high_ref, *out_refs):
    low = pl.program_id(0) < pl.num_programs(0) // 2
    group, rows, _ = low_ref.shape
    at = 0
    for out_ref in out_refs:
        width = out_ref.shape[1]
        for source, chosen in [(low_ref, low), (high_ref, jnp.logical_not(low))]:

            @pl.when(chosen)
            def _():
                for slot in range(group):
                    place = (index[0] % group) ^ slot
                    place = pl.multiple_of(place * rows, rows)
                    out_ref[pl.ds(place, rows), :] = source[slot, :, at : at + width].astype(F32)

        at += width


def unpack(low, high, order, widths):
    count, rows, columns = low.shape
    group = min(4, count)
    steps = 2 * count // group
    place = lambda j, index: (jnp.bitwise_xor(index[0] // group, j), 0)
    return kernel_call(
        unpack_kernel,
        grid_spec=pltpu.PrefetchScalarGridSpec(
            num_scalar_prefetch=1,
            grid=(steps,),
            in_specs=[
                pl.BlockSpec(
                    (group, rows, columns), lambda j, i: (jnp.minimum(j, steps // 2 - 1), 0, 0)
                ),
                pl.BlockSpec(
                    (group, rows, columns), lambda j, i: (jnp.maximum(j - steps // 2, 0), 0, 0)
                ),
            ],
            out_specs=[pl.BlockSpec((group * rows, width), place) for width in widths],
        ),
        out_shape=[jax.ShapeDtypeStruct((2 * count * rows, width), F32) for width in widths],
        compiler_params=pltpu.CompilerParams(vmem_limit_bytes=24 << 20),
        cost_estimate=lasting(5),
        name="unpack",
    )(piece_index(order).reshape(1), low, high)


def shards(
    frames,
    clip_lengths,
    text_states,
    text_segments,
    gain_one,
    shift_one,
    gain_two,
    shift_two,
    gain_three,
    shift_three,
    query_weight,
    key_weight,
    value_weight,
    output_weight,
    cross_query,
    cross_key,
    cross_value,
    cross_output,
    inner_weight,
    outer_weight,
    cotangent,
):
    row_count, depth = frames.shape
    width_here = query_weight.shape[1]
    heads_here = width_here // HEAD_DIM
    blk_count, tp_count = lax.axis_size("blk"), lax.axis_size("tp")
    blk, tp = lax.axis_index("blk"), lax.axis_index("tp")
    core = blk % 2
    copies = blk_count // heads_here
    sub = row_count // copies
    half = row_count // tp_count
    mine = blk % copies
    scale = float(HEAD_DIM) ** (-0.5)
    bits = [1 << i for i in range(1, blk_count.bit_length() - 1)]
    order_one = [1] + bits
    order_two = [1, bits[1], bits[0]] + bits[2:]

    def own_rows(array):
        return lax.dynamic_slice_in_dim(array, tp * half, half, 0)

    def other_rows(array):
        return lax.dynamic_slice_in_dim(array, (1 - tp) * half, half, 0)

    row = lambda array: array.reshape(1, -1)
    qkv_weights = [query_weight, key_weight, value_weight]
    if sub % 128 == 0:
        normed_one, qkv = embed(
            frames, row(gain_one), row(shift_one), qkv_weights, blk_count, sub, scale
        )
    else:
        hat, _ = normalize(frames.astype(F32))
        normed_one = (hat * gain_one + shift_one).astype(BF)
        qkv = jnp.stack([dg(weight, normed_one, ((0,), (1,))) for weight in qkv_weights])
        qkv = (qkv * jnp.array([scale, 1.0, 1.0], F32)[:, None, None]).astype(BF)
        qkv = qkv.reshape(3, heads_here, HEAD_DIM, copies, sub).transpose(1, 3, 0, 2, 4)
        qkv = qkv.reshape(blk_count, 3, HEAD_DIM, sub)

    weights_two = [output_weight, cross_query, cross_output]
    hops = [first_hop(w, core) for w in after(weights_two, qkv)]
    text_k = dg(cross_key, text_states, ((0,), (1,))).astype(BF)
    text_v = dg(cross_value, text_states, ((0,), (1,))).astype(BF)
    text_own = jnp.stack([text_k, text_v])
    text_both = jnp.stack([text_own, over_x(text_own)], axis=1)

    def bring_heads(array):
        got = lax.all_to_all(array, "blk", 0, 0, tiled=True)
        return got.reshape(heads_here, copies, array.shape[1], HEAD_DIM, sub)

    got = lax.all_to_all(qkv, "blk", 0, 0, tiled=True)
    queries = got[:, 0].transpose(1, 0, 2).reshape(HEAD_DIM, blk_count * sub)
    both = got[:, 1:][:, :, :, None, :]
    bit = 1
    while bit < copies:
        both = jnp.concatenate([both, over_blk(both, bit)], axis=3)
        bit *= 2
    both = both.transpose(1, 2, 0, 3, 4).reshape(2, HEAD_DIM, blk_count * row_count)
    keys, values = both[0], both[1]
    rows_all = jnp.arange(blk_count, dtype=jnp.int32)[:, None] * row_count
    rows_all = (rows_all + mine * sub + jnp.arange(sub, dtype=jnp.int32)[None, :]).reshape(-1)
    _, first = clip_rows(rows_all, clip_lengths)
    flip = mine * sub
    out, log_total = attend(queries, keys, values, rows_all, first, flip)
    hops, out = lax.optimization_barrier((hops, out))
    output_both, query_both, cross_both = [
        list(pair) for pair in zip(weights_two, weld(hops, [over_blk(h, 1) for h in hops], core))
    ]

    out_low = out.astype(BF).reshape(HEAD_DIM, blk_count, sub).transpose(1, 0, 2)[:, None]
    attended = bring_heads(out_low)[:, :, 0]

    attended, output_both, query_both, cross_both = lax.optimization_barrier(
        (attended, output_both, query_both, cross_both)
    )

    def token_half(array, which):
        array = array.reshape(heads_here, tp_count, copies // tp_count, HEAD_DIM, sub)
        array = lax.dynamic_index_in_dim(array, which, 1, keepdims=False)
        return array.transpose(0, 2, 1, 3).reshape(width_here, half)

    a_own, a_sent = token_half(attended, tp), token_half(attended, 1 - tp)
    a_both = [a_own, over_x(a_sent)]

    rows = blk * row_count + tp * half + jnp.arange(half, dtype=jnp.int32)
    segment, _ = clip_rows(rows, clip_lengths)
    x_low = own_rows(frames)
    norms = [row(gain_two), row(shift_two), row(gain_three), row(shift_three)]
    segment, text_segment = segment.reshape(1, -1), text_segments.reshape(-1, 1)
    first_sum, second_sum, h2_own, h3_own, qc_t, oc_t, c_own, c_sent = cross_forward(
        a_both, x_low, norms, output_both, query_both, cross_both,
        text_both[0], text_both[1], segment, text_segment, scale,
    )

    h3_other = over_x(h3_own)
    hidden, grad_pre, dh3_own, dh3_sent = hidden_pass(
        h3_own, h3_other, cotangent, inner_weight, outer_weight, tp
    )
    dh3_got = over_x(dh3_sent)
    hidden_both, y_kept, y_sent = hidden_grads(
        h3_own, h3_other, cotangent, hidden, grad_pre, outer_weight, tp
    )
    hidden_piece = lax.psum_scatter(hidden_both, "blk", scatter_dimension=0, tiled=True)
    dh3_got, y_kept = lax.optimization_barrier((dh3_got, y_kept))

    dx1, dx1_low, dx2_low, dqc_own, dqc_sent, da_own, da_sent, text_own, text_sent, small_cross = cross_backward(
        dh3_own, dh3_got, own_rows(cotangent), first_sum, second_sum, row(gain_two),
        row(gain_three), output_both, query_both, cross_both, text_both[0], text_both[1],
        qc_t, oc_t, segment, text_segment, scale,
    )
    da_other = over_x(da_sent)
    da_own = after(da_own, da_other)

    def as_heads(array):
        return array.reshape(heads_here, HEAD_DIM, copies // tp_count, sub).transpose(0, 2, 1, 3)

    low = jnp.where(tp == 0, as_heads(da_own), as_heads(da_other))
    high = jnp.where(tp == 0, as_heads(da_other), as_heads(da_own))
    sent = jnp.concatenate([low, high], axis=1).reshape(blk_count, 1, HEAD_DIM, sub)
    grads = lax.all_to_all(sent, "blk", 0, 0, tiled=True)[:, 0]
    grads = grads.transpose(1, 0, 2).reshape(HEAD_DIM, blk_count * sub)
    dx1_other, dx2_other, dqc_other, c_other = [
        over_x(value) for value in after((dx1_low, dx2_low, dqc_sent, c_sent), da_other)
    ]
    grads, dx1_other, dx2_other, dqc_other, c_other = lax.optimization_barrier(
        (grads, dx1_other, dx2_other, dqc_other, c_other)
    )
    dq, parts = attend_back(
        queries, keys, values, rows_all, first, flip, out, log_total, grads, sub
    )
    while parts.shape[0] > 2:
        got = over_blk(halves(parts, 1), parts.shape[0] // 2)
        parts = (halves(parts, 0).astype(F32) + got.astype(F32)).astype(BF)
    parts_got = over_blk(parts[1], 1)
    sent = combine(dq, parts, parts_got, scale)
    back = bring_heads(sent)
    text_got, h2_other, y_got = after(
        [over_x(value) for value in after((text_sent, h2_own, y_sent), da_other)], sent
    )
    text_part = text_own + text_got.astype(F32)
    pair_send, pair_keep = pair_grads(
        [
            (a_own, a_sent, dx1_low, dx1_other),
            (c_own, c_other, dx2_low, dx2_other),
            (dqc_own, dqc_other, h2_own, h2_other),
        ],
        core,
    )
    y_own = (second_sum + y_kept + y_got.astype(F32)).astype(BF)
    back, pair_send = lax.optimization_barrier((back, pair_send))
    back = back.transpose(2, 0, 3, 1, 4).reshape(3, width_here, row_count)
    dh1_own, dh1_sent = project_back(back, [query_weight, key_weight, value_weight], tp)
    dh1_got = over_x(dh1_sent)
    head_send, head_keep = head_grads(back, normed_one, core)
    head_send, hidden_piece = lax.optimization_barrier((head_send, hidden_piece))
    hidden_both = lax.all_gather(hidden_piece, "blk", axis=0, tiled=True)
    pairs = Stream(pair_send, pair_keep, order_one, blk)
    heads = Stream(head_send, head_keep, order_two, blk)
    text = Butterfly(text_part, order_one, BF)
    y_other = over_x(y_own)
    streams = [pairs, heads, text]
    dh1_got, y_other = meet(streams, (dh1_got, y_other))
    result = in_order(y_own, y_other, tp)
    step_together([pairs, heads])
    text.step()
    through, grad_gain_one, grad_shift_one = norm_back(
        x_low.astype(F32), gain_one, dh1_own + dh1_got.astype(F32)
    )
    dx = (dx1 + through).astype(BF)
    dx_other = over_x(dx)
    small = jnp.concatenate([grad_gain_one[None], grad_shift_one[None], small_cross])
    small_got = over_x(small)
    dx_other, small_got = meet(streams, (dx_other, small_got))
    grad_frames = in_order(dx, dx_other, tp)
    small = Butterfly(small + small_got, order_one, F32)
    while pairs.phase < len(order_one) - 1:
        step_together([pairs, heads])
        text.step()
        meet(streams + [small], ())
        small.step()
    pieces = lax.all_gather(last_halves(heads, pairs), "blk")
    while small.phase is not None or text.phase is not None:
        small.step()
        text.step()
        meet([small, text], ())
    text_total = text.value.astype(BF)
    grad_text = dg(text_total[0], cross_key, ((0,), (1,)))
    grad_text = (grad_text + dg(text_total[1], cross_value, ((0,), (1,)))).astype(BF)
    text_got = over_x(grad_text)
    grad_cross_key = dg(text_states, text_total[0], ((0,), (1,)))
    grad_cross_value = dg(text_states, text_total[1], ((0,), (1,)))
    grad_text = grad_text.astype(F32) + text_got.astype(F32)
    grad_text, grad_cross_key, grad_cross_value, hidden_both = lax.optimization_barrier(
        (grad_text, grad_cross_key, grad_cross_value, hidden_both)
    )
    grad_outer, grad_inner = hidden_out(hidden_both)
    grads = widen(
        after(pieces, grad_inner), order_two, order_one, heads.keep.shape[0], pairs.keep.shape[0],
        width_here, depth,
    )
    grad_query, grad_key, grad_value, grad_output, grad_cross_output, grad_cross_query = grads
    small = small.value

    return (
        result,
        grad_frames,
        grad_text,
        small[0],
        small[1],
        small[2],
        small[3],
        small[4],
        small[5],
        grad_query,
        grad_key,
        grad_value,
        grad_output,
        grad_cross_query,
        grad_cross_key,
        grad_cross_value,
        grad_cross_output,
        grad_inner,
        grad_outer,
    )


def solution(mesh):
    return jax.shard_map(
        shards,
        mesh=mesh,
        in_specs=(
            P("blk", None),
            P(),
            P(),
            P(),
            P(),
            P(),
            P(),
            P(),
            P(),
            P(),
            P(None, "tp"),
            P(None, "tp"),
            P(None, "tp"),
            P("tp", None),
            P(None, "tp"),
            P(None, "tp"),
            P(None, "tp"),
            P("tp", None),
            P(None, "tp"),
            P("tp", None),
            P("blk", None),
        ),
        out_specs=(
            P("blk", None),
            P("blk", None),
            P(),
            P(),
            P(),
            P(),
            P(),
            P(),
            P(),
            P(None, "tp"),
            P(None, "tp"),
            P(None, "tp"),
            P("tp", None),
            P(None, "tp"),
            P(None, "tp"),
            P(None, "tp"),
            P("tp", None),
            P(None, "tp"),
            P("tp", None),
        ),
        check_vma=False,
    )
```

profile of v0, /device:TPU:0, one launch (start us, length us, event | category | flops | bytes accessed | tf_op | source)
XLA Modules:
  0.0 453.2 jit_solution(13745557848143320082)
XLA Ops:
  13.4 2.2 embed.1
  16.4 7.6 %all-to-all-start = ((bf16[16,3,64,128]{3,2,1,0:T(8,128)(2,1)}), bf16[16,3,64,128]{3,2,1,0:T(8,128)(2,1)}, u32[]{:S(2)}, u32[]{:S(2)}) async-start(bf16[16,3,64,128]{3,2,1,0:T(8,128)(2,1)} %get-tuple-element.139), calls=%async_computation | async-start | bytes 1572864 | tf_op jit(solution)/shard_map/all_to_all | solution.py:1165
  24.0 1.9 constant_dynamic-slice_fusion.4
  32.9 9.9 %all-to-all-done = bf16[16,3,64,128]{3,2,1,0:T(8,128)(2,1)} async-done(((bf16[16,3,64,128]{3,2,1,0:T(8,128)(2,1)}), bf16[16,3,64,128]{3,2,1,0:T(8,128)(2,1)}, u32[]{:S(2)}, u32[]{:S(2)}) %all-to-all-start) | async-done | bytes 786464 | tf_op jit(solution)/shard_map/all_to_all | solution.py:1165
  47.7 1.6 copy.139
  49.7 15.3 %attend.1 = (f32[64,2048]{1,0:T(8,128)S(1)}, f32[1,2048]{1,0:T(1,128)S(1)}) custom-call(s32[4,4]{1,0:T(4,128)S(1)} %pad_add_fusion.ranges, s32[1]{0:T(128)} %bitcast.7.flips, bf16[64,2048]{1,0:T(8,128)(2,1)S(1)} %copy_bitcast_fusion.2.q_ref, bf16[64,4096]{1,0:T(8,128)(2,1)S(1)} %squeeze.53.k_ref, bf16[64,4096]{1,0:T(8,128)(2,1)S(1)} %squeeze.54.v_ref, ...), custom_call_target="tpu_custom_call" | custom-call | bytes 55500000 | tf_op jit(solution)/shard_map/attend/pallas_call | solution.py:29
  66.6 5.5 %all-to-all-start.1 = ((bf16[16,1,64,128]{3,2,1,0:T(8,128)(2,1)}), bf16[16,1,64,128]{3,2,1,0:T(8,128)(2,1)}, u32[]{:S(2)}, u32[]{:S(2)}) async-start(bf16[16,1,64,128]{3,2,1,0:T(8,128)(2,1)} %bitcast_bitcast_fusion), calls=%async_computation.1 | async-start | bytes 524288 | tf_op jit(solution)/shard_map/all_to_all | solution.py:1162
  73.3 1.7 fusion.2
  78.0 3.7 weld.1
  82.2 1.7 constant_dynamic-slice_fusion.2
  85.6 2.0 fusion.19
  87.6 1.6 collective-permute-done.7.a_other
  89.9 9.4 %cross_forward.1 = (f32[128,1024]{1,0:T(8,128)}, f32[128,1024]{1,0:T(8,128)}, bf16[128,1024]{1,0:T(8,128)(2,1)}, bf16[128,1024]{1,0:T(8,128)(2,1)}, bf16[2,512,1...) custom-call(bf16[512,128]{1,0:T(8,128)(2,1)} %bitcast.131, ...), custom_call_target="tpu_custom_call" | custom-call | bytes 25900000 | tf_op jit(solution)/shard_map/cross_forward/pallas_call | solution.py:29
  99.3 1.6 collective-permute-start.9
  100.9 5.9 %collective-permute-done.9.h_other = bf16[128,1024]{1,0:T(8,128)(2,1)S(1)} collective-permute-done((bf16[128,1024]{1,0:T(8,128)(2,1)}, bf16[128,1024]{1,0:T(8,128)(2,1)S(1)}, u32[]{:S(2)}, u32[]{:S(2)}) %collective-permute-start.9) | collective-permute-done | bytes 262176 | tf_op jit(solution)/shard_map/ppermute | solution.py:245
  107.8 8.4 %hidden_pass.1 = (bf16[256,2048]{1,0:T(8,128)(2,1)S(1)}, bf16[256,2048]{1,0:T(8,128)(2,1)S(1)}, f32[128,1024]{1,0:T(8,128)S(1)}, bf16[128,1024]{1,0:T(8,128)(2,1)S(1)}) custom-call(s32[1]{0:T(128)} %bitcast.33.tp_ref.place.tp, bf16[128,1024]{1,0:T(8,128)(2,1)S(1)} %copy-done.12, bf16[128,1024]{1,0:T(8,128)(2,1)S(1)} %collective-permute-done.9.h_other, ...), custom_call_target="tpu_custom_call" | custom-call | bytes 37000000 | tf_op jit(solution)/shard_map/hidden_pass/pallas_call | solution.py:29
  116.2 7.4 %hidden_grads.1 = (bf16[2048,2048]{1,0:T(8,128)(2,1)}, f32[128,1024]{1,0:T(8,128)}, bf16[128,1024]{1,0:T(8,128)(2,1)}) custom-call(s32[1]{0:T(128)} %bitcast.33.tp_ref.place.tp, bf16[128,1024]{1,0:T(8,128)(2,1)S(1)} %copy-done.12, bf16[128,1024]{1,0:T(8,128)(2,1)S(1)} %collective-permute-done.9.h_other, bf16[256,1024]{1,0:T(8,128)(2,1)S(1)} %copy-done.6, ...), custom_call_target="tpu_custom_call" | custom-call | bytes 33300000 | tf_op jit(solution)/shard_map/hidden_grads/pallas_call | solution.py:29
  126.8 4.1 collective-permute-done.10.dh_got
  131.7 11.9 %cross_backward.1 = (f32[128,1024]{1,0:T(8,128)}, bf16[128,1024]{1,0:T(8,128)(2,1)}, bf16[128,1024]{1,0:T(8,128)(2,1)}, bf16[512,128]{1,0:T(8,128)(2,1)}, bf16[5...) custom-call(f32[128,1024]{1,0:T(8,128)} %copy-done.14, ...), custom_call_target="tpu_custom_call" | custom-call | bytes 33300000 | tf_op jit(solution)/shard_map/cross_backward/pallas_call | solution.py:29
  143.6 1.5 collective-permute-start.11
  145.1 3.7 collective-permute-done.11
  150.5 6.0 %all-to-all-start.2 = ((bf16[16,1,64,128]{3,2,1,0:T(8,128)(2,1)}), bf16[16,1,64,128]{3,2,1,0:T(8,128)(2,1)S(1)}, u32[]{:S(2)}, u32[]{:S(2)}) async-start(bf16[16,1,64,128]{3,2,1,0:T(8,128)(2,1)} %bitcast.36), calls=%async_computation.2 | async-start | bytes 524288 | tf_op jit(solution)/shard_map/all_to_all | solution.py:1234
  160.7 10.4 %all-to-all-done.2 = bf16[16,1,64,128]{3,2,1,0:T(8,128)(2,1)S(1)} async-done(((bf16[16,1,64,128]{3,2,1,0:T(8,128)(2,1)}), bf16[16,1,64,128]{3,2,1,0:T(8,128)(2,1)S(1)}, u32[]{:S(2)}, u32[]{:S(2)}) %all-to-all-start.2) | async-done | bytes 262176 | tf_op jit(solution)/shard_map/all_to_all | solution.py:1234
  171.6 5.3 %collective-permute-done.16.refs_7_ = bf16[128,1024]{1,0:T(8,128)(2,1)} collective-permute-done((bf16[128,1024]{1,0:T(8,128)(2,1)S(1)}, bf16[128,1024]{1,0:T(8,128)(2,1)}, u32[]{:S(2)}, u32[]{:S(2)}) %collective-permute-start.16) | collective-permute-done | bytes 262176 | tf_op jit(solution)/shard_map/ppermute | solution.py:245
  178.0 17.4 %attend_back.1 = (bf16[16,64,128]{2,1,0:T(8,128)(2,1)S(1)}, bf16[2,16,2,64,128]{4,3,2,1,0:T(8,128)(2,1)S(1)}) custom-call(s32[4,4]{1,0:T(4,128)S(1)} %pad_add_fusion.ranges, s32[1]{0:T(128)} %bitcast.7.flips, bf16[64,2048]{1,0:T(8,128)(2,1)S(1)} %copy_bitcast_fusion.2.q_ref, bf16[64,4096]{1,0:T(8,128)(2,1)S(1)} %squeeze.53.k_ref, ...), custom_call_target="tpu_custom_call" | custom-call | bytes 62900000 | tf_op jit(solution)/shard_map/attend_back/pallas_call | solution.py:29
  196.2 1.9 collective-permute-done.19.got_ref
  198.9 3.5 combine.1
  202.4 5.7 %all-to-all-start.3 = ((bf16[16,3,64,128]{3,2,1,0:T(8,128)(2,1)}), bf16[16,3,64,128]{3,2,1,0:T(8,128)(2,1)S(1)}, u32[]{:S(2)}, u32[]{:S(2)}) async-start(bf16[16,3,64,128]{3,2,1,0:T(8,128)(2,1)} %combine.1), calls=%async_computation.3 | async-start | bytes 1572864 | tf_op jit(solution)/shard_map/all_to_all | solution.py:1162
  210.8 6.7 %collective-permute-done.12 = bf16[2,512,128]{2,1,0:T(8,128)(2,1)S(1)} collective-permute-done((bf16[2,512,128]{2,1,0:T(8,128)(2,1)}, bf16[2,512,128]{2,1,0:T(8,128)(2,1)S(1)}, u32[]{:S(2)}, u32[]{:S(2)}) %collective-permute-start.12) | collective-permute-done | bytes 262176 | tf_op jit(solution)/shard_map/ppermute | solution.py:245
  217.6 5.6 %collective-permute-done.13.refs_11_ = bf16[128,1024]{1,0:T(8,128)(2,1)S(1)} collective-permute-done((bf16[128,1024]{1,0:T(8,128)(2,1)S(1)}, bf16[128,1024]{1,0:T(8,128)(2,1)S(1)}, u32[]{:S(2)}, u32[]{:S(2)}) %collective-permute-start.13) | collective-permute-done | bytes 262176 | tf_op jit(solution)/shard_map/ppermute | solution.py:245
  223.2 5.1 %collective-permute-done.14 = bf16[128,1024]{1,0:T(8,128)(2,1)S(1)} collective-permute-done((bf16[128,1024]{1,0:T(8,128)(2,1)}, bf16[128,1024]{1,0:T(8,128)(2,1)S(1)}, u32[]{:S(2)}, u32[]{:S(2)}) %collective-permute-start.14) | collective-permute-done | bytes 262176 | tf_op jit(solution)/shard_map/ppermute | solution.py:245
  228.3 4.9 %pair_grads.1 = (bf16[256,3072]{1,0:T(8,128)(2,1)}, bf16[256,3072]{1,0:T(8,128)(2,1)}) custom-call(s32[1]{0:T(128)} %bitcast.17.core, bf16[512,128]{1,0:T(8,128)(2,1)} %bitcast.132, bf16[512,128]{1,0:T(8,128)(2,1)} %bitcast.134, bf16[128,1024]{1,0:T(8,128)(2,1)} %get-tuple-element.184.refs_2_, bf16[128,1024]{1,0:T(8,128)(2,1)} %copy-done.45, ...), custom_call_target="tpu_custom_call" | custom-call | bytes 14800000 | tf_op jit(solution)/shard_map/pair_grads/pallas_call | solution.py:29
  236.1 3.7 head_grads.1
  239.8 7.2 %reduce-scatter.2.cloned.1.call-done = bf16[128,2048]{1,0:T(8,128)(2,1)} async-done(((bf16[2048,2048]{1,0:T(8,128)(2,1)}), bf16[128,2048]{1,0:T(8,128)(2,1)}) %reduce-scatter.2.cloned.1.call-update) | async-done | bytes 524304 | tf_op jit(solution)/shard_map/reduce_scatter | solution.py:1217
  250.1 4.0 project_back.1
  255.7 3.0 collective-permute-done.24
  258.7 5.1 %collective-permute-done.23 = bf16[128,1024]{1,0:T(8,128)(2,1)S(1)} collective-permute-done((bf16[128,1024]{1,0:T(8,128)(2,1)}, bf16[128,1024]{1,0:T(8,128)(2,1)S(1)}, u32[]{:S(2)}, u32[]{:S(2)}) %collective-permute-start.23) | collective-permute-done | bytes 262176 | tf_op jit(solution)/shard_map/ppermute | solution.py:245
  263.8 6.2 %fold.3 = (bf16[128,3072]{1,0:T(8,128)(2,1)}, bf16[128,3072]{1,0:T(8,128)(2,1)}, bf16[256,1536]{1,0:T(8,128)(2,1)}, bf16[256,1536]{1,0:T(8,128)(2,1)}) custom-call(s32[2]{0:T(128)S(1)} %get-tuple-element.373.sides, bf16[256,3072]{1,0:T(8,128)(2,1)} %get-tuple-element.213.refs_0_, bf16[256,3072]{1,0:T(8,128)(2,1)} %collective-permute-done.20.refs_1_, ...), custom_call_target="tpu_custom_call" | custom-call | bytes 11100000 | tf_op jit(solution)/shard_map/fold/pallas_call | solution.py:29
  270.0 1.5 collective-permute-start.25
  271.6 3.1 collective-permute-start.26
  276.0 1.8 collective-permute-start.29
  277.7 5.3 %collective-permute-done.29 = f32[6,1024]{1,0:T(8,128)S(1)} collective-permute-done((f32[6,1024]{1,0:T(8,128)S(1)}, f32[6,1024]{1,0:T(8,128)S(1)}, u32[]{:S(2)}, u32[]{:S(2)}) %collective-permute-start.29) | collective-permute-done | bytes 24608 | tf_op jit(solution)/shard_map/ppermute | solution.py:245
  283.0 23.0 %collective-permute-done.27 = bf16[2,512,128]{2,1,0:T(8,128)(2,1)S(1)} collective-permute-done((bf16[2,512,128]{2,1,0:T(8,128)(2,1)S(1)}, bf16[2,512,128]{2,1,0:T(8,128)(2,1)S(1)}, u32[]{:S(2)}, u32[]{:S(2)}) %collective-permute-start.27) | collective-permute-done | bytes 262176 | tf_op jit(solution)/shard_map/ppermute | solution.py:249
  306.1 2.5 collective-permute-done.26.refs_3_
  309.4 4.9 %fold.4 = (bf16[64,3072]{1,0:T(8,128)(2,1)}, bf16[64,3072]{1,0:T(8,128)(2,1)}, bf16[128,1536]{1,0:T(8,128)(2,1)}, bf16[128,1536]{1,0:T(8,128)(2,1)}) custom-call(s32[2]{0:T(128)S(1)} %get-tuple-element.374.sides, bf16[128,3072]{1,0:T(8,128)(2,1)} %get-tuple-element.223.refs_0_, bf16[128,3072]{1,0:T(8,128)(2,1)} %copy-done.35, ...), custom_call_target="tpu_custom_call" | custom-call | bytes 11100000 | tf_op jit(solution)/shard_map/fold/pallas_call | solution.py:29
  314.3 2.0 collective-permute-start.30
  316.3 2.5 collective-permute-start.31
  321.0 21.2 %collective-permute-done.32 = bf16[2,512,128]{2,1,0:T(8,128)(2,1)S(1)} collective-permute-done((bf16[2,512,128]{2,1,0:T(8,128)(2,1)}, bf16[2,512,128]{2,1,0:T(8,128)(2,1)S(1)}, u32[]{:S(2)}, u32[]{:S(2)}) %collective-permute-start.32) | collective-permute-done | bytes 262176 | tf_op jit(solution)/shard_map/ppermute | solution.py:249
  342.3 2.5 collective-permute-start.36
  344.9 4.2 fold.5
  349.8 2.3 collective-permute-start.35
  353.1 3.0 collective-permute-done.37
  356.1 11.7 %collective-permute-done.34.pair_got = bf16[32,3072]{1,0:T(8,128)(2,1)S(1)} collective-permute-done((bf16[32,3072]{1,0:T(8,128)(2,1)}, bf16[32,3072]{1,0:T(8,128)(2,1)S(1)}, u32[]{:S(2)}, u32[]{:S(2)}) %collective-permute-start.34) | collective-permute-done | bytes 196640 | tf_op jit(solution)/shard_map/ppermute | solution.py:249
  367.7 3.4 collective-permute-done.35.head_got
  371.9 2.1 last_halves.1
  378.6 4.3 collective-permute-start.38
  382.9 2.4 collective-permute-start.40
  385.3 1.7 convolution_bitcast_fusion.1
  387.0 2.2 collective-permute-done.40
  390.8 2.9 copy.148
  393.6 1.8 copy.149
  395.5 10.7 %hidden_out.1 = (f32[2048,1024]{1,0:T(8,128)}, f32[1024,2048]{1,0:T(8,128)}) custom-call(bf16[2048,2048]{1,0:T(8,128)(2,1)} %all-gather.4.cloned.1.call-done.both_ref), custom_call_target="tpu_custom_call" | custom-call | bytes 33300000 | tf_op jit(solution)/shard_map/hidden_out/pallas_call | solution.py:29
  406.1 31.8 %all-gather.6.cloned.1.call-done = bf16[2048,1536]{1,0:T(8,128)(2,1)} async-done(((bf16[128,1536]{1,0:T(8,128)(2,1)}), bf16[2048,1536]{1,0:T(8,128)(2,1)}) %all-gather.6.cloned.1.call-update) | async-done | bytes 6291472 | tf_op jit(solution)/shard_map/all_gather | solution.py:1295
  437.9 8.3 %widen.1 = (f32[1024,512]{1,0:T(8,128)}, f32[1024,512]{1,0:T(8,128)}, f32[1024,512]{1,0:T(8,128)}, f32[512,1024]{1,0:T(8,128)}, f32[512,1024]{1,0:T(8,128)}, /*index=5*/f32[1024,512]{1,0:T(8,128)}) custom-call(s32[2,16]{1,0:T(2,128)S(1)} %copy-done.23, bf16[16,128,1536]{2,1,0:T(8,128)(2,1)} %bitcast.121, bf16[16,128,1536]{2,1,0:T(8,128)(2,1)} %bitcast.122, ...), custom_call_target="tpu_custom_call" | custom-call | bytes 25900000 | tf_op jit(solution)/shard_map/widen/pallas_call | solution.py:29
  (252 shorter events, 64.6 us)
Async XLA Ops:
  7.2 25.1 %copy-start = (bf16[1024,512]{1,0:T(8,128)(2,1)S(1)}, bf16[1024,512]{1,0:T(8,128)(2,1)}, u32[]{:S(2)}) copy-start(bf16[1024,512]{1,0:T(8,128)(2,1)} %param.37) | copy-start | bytes 3145732
  16.4 12.3 %copy-start.27 = (bf16[1024,512]{1,0:T(8,128)(2,1)S(1)}, bf16[1024,512]{1,0:T(8,128)(2,1)}, u32[]{:S(2)}) copy-start(bf16[1024,512]{1,0:T(8,128)(2,1)} %wq_own.1) | copy-start | bytes 3145732
  16.4 14.7 %copy-start.59 = (s32[8]{0:T(128)S(1)}, s32[8]{0:T(128)}, u32[]{:S(2)}) copy-start(s32[8]{0:T(128)} %param.23) | copy-start | bytes 100
  16.4 15.9 %copy-start.29 = (bf16[128,1024]{1,0:T(8,128)(2,1)S(1)}, bf16[128,1024]{1,0:T(8,128)(2,1)}, u32[]{:S(2)}) copy-start(bf16[128,1024]{1,0:T(8,128)(2,1)} %param.24) | copy-start | bytes 786436
  16.4 26.4 %all-to-all-start = ((bf16[16,3,64,128]{3,2,1,0:T(8,128)(2,1)}), bf16[16,3,64,128]{3,2,1,0:T(8,128)(2,1)}, u32[]{:S(2)}, u32[]{:S(2)}) async-start(bf16[16,3,64,128]{3,2,1,0:T(8,128)(2,1)} %get-tuple-element.139), calls=%async_computation | async-start | bytes 1572864 | tf_op jit(solution)/shard_map/all_to_all | solution.py:1165
  25.9 39.1 %collective-permute-start.2 = (bf16[256,1024]{1,0:T(8,128)(2,1)}, bf16[256,1024]{1,0:T(8,128)(2,1)}, u32[]{:S(2)}, u32[]{:S(2)}) collective-permute-start(bf16[256,1024]{1,0:T(8,128)(2,1)} %constant_dynamic-slice_fusion.4), channel_id=1, source_target_pairs={{0,1},{1,0},{2,3},{3,2},{4,5},{5,4},{6,7},{7,6},{8,9},{9,8},{10,11... | collective-permute-start | bytes 1572872 | tf_op jit(solution)/shard_map/ppermute | solution.py:245
  28.2 36.8 %collective-permute-start = (bf16[256,1024]{1,0:T(8,128)(2,1)}, bf16[256,1024]{1,0:T(8,128)(2,1)}, u32[]{:S(2)}, u32[]{:S(2)}) collective-permute-start(bf16[256,1024]{1,0:T(8,128)(2,1)} %constant_dynamic-slice_fusion.6), channel_id=1, source_target_pairs={{0,1},{1,0},{2,3},{3,2},{4,5},{5,4},{6,7},{7,6},{8,9},{9,8},{10,11... | collective-permute-start | bytes 1572872 | tf_op jit(solution)/shard_map/ppermute | solution.py:245
  29.6 35.5 %collective-permute-start.1 = (bf16[512,512]{1,0:T(8,128)(2,1)}, bf16[512,512]{1,0:T(8,128)(2,1)}, u32[]{:S(2)}, u32[]{:S(2)}) collective-permute-start(bf16[512,512]{1,0:T(8,128)(2,1)} %constant_dynamic-slice_fusion.5), channel_id=1, source_target_pairs={{0,1},{1,0},{2,3},{3,2},{4,5},{5,4},{6,7},{7,6},{8,9},{9,8},{10,11... | collective-permute-start | bytes 1572872 | tf_op jit(solution)/shard_map/ppermute | solution.py:245
  43.8 2.0 collective-permute-start.3
  66.6 15.6 %all-to-all-start.1 = ((bf16[16,1,64,128]{3,2,1,0:T(8,128)(2,1)}), bf16[16,1,64,128]{3,2,1,0:T(8,128)(2,1)}, u32[]{:S(2)}, u32[]{:S(2)}) async-start(bf16[16,1,64,128]{3,2,1,0:T(8,128)(2,1)} %bitcast_bitcast_fusion), calls=%async_computation.1 | async-start | bytes 524288 | tf_op jit(solution)/shard_map/all_to_all | solution.py:1162
  72.1 174.9 %reduce-scatter.2.cloned.1.call-start = ((), (), s32[]{:S(2)}) async-start(), calls=%async_computation.5 | async-start | bytes 8912896 | tf_op jit(solution)/shard_map/reduce_scatter | solution.py:1217
  72.3 5.6 %collective-permute-start.4 = (bf16[256,1024]{1,0:T(8,128)(2,1)}, bf16[256,1024]{1,0:T(8,128)(2,1)}, u32[]{:S(2)}, u32[]{:S(2)}) collective-permute-start(bf16[256,1024]{1,0:T(8,128)(2,1)} %collective-permute-done.refs_0_), channel_id=1, source_target_pairs={{0,2},{2,0},{4,6},{6,4},{8,10},{10,8},{12,14},{14,12},{16,18},{18,... | collective-permute-start | bytes 1572872 | tf_op jit(solution)/shard_map/ppermute | solution.py:249
  72.8 5.2 %collective-permute-start.5 = (bf16[512,512]{1,0:T(8,128)(2,1)}, bf16[512,512]{1,0:T(8,128)(2,1)}, u32[]{:S(2)}, u32[]{:S(2)}) collective-permute-start(bf16[512,512]{1,0:T(8,128)(2,1)} %collective-permute-done.1.refs_1_), channel_id=1, source_target_pairs={{0,2},{2,0},{4,6},{6,4},{8,10},{10,8},{12,14},{14,12},{16,18},{18,... | collective-permute-start | bytes 1572872 | tf_op jit(solution)/shard_map/ppermute | solution.py:249
  72.9 5.1 %collective-permute-start.6 = (bf16[256,1024]{1,0:T(8,128)(2,1)}, bf16[256,1024]{1,0:T(8,128)(2,1)}, u32[]{:S(2)}, u32[]{:S(2)}) collective-permute-start(bf16[256,1024]{1,0:T(8,128)(2,1)} %collective-permute-done.2.refs_2_), channel_id=1, source_target_pairs={{0,2},{2,0},{4,6},{6,4},{8,10},{10,8},{12,14},{14,12},{16,18},{18,... | collective-permute-start | bytes 1572872 | tf_op jit(solution)/shard_map/ppermute | solution.py:249
  75.7 9.9 %collective-permute-start.8 = (bf16[2,512,128]{2,1,0:T(8,128)(2,1)}, bf16[2,512,128]{2,1,0:T(8,128)(2,1)}, u32[]{:S(2)}, u32[]{:S(2)}) collective-permute-start(bf16[2,512,128]{2,1,0:T(8,128)(2,1)} %get-tuple-element.359), channel_id=1, source_target_pairs={{0,1},{1,0},{2,3},{3,2},{4,5},{5,4},{6,7},{7,6},{8,9},{9,8},{10,11... | collective-permute-start | bytes 786440 | tf_op jit(solution)/shard_map/ppermute | solution.py:245
  82.2 24.6 %copy-start.6 = (bf16[256,1024]{1,0:T(8,128)(2,1)S(1)}, bf16[256,1024]{1,0:T(8,128)(2,1)}, u32[]{:S(2)}) copy-start(bf16[256,1024]{1,0:T(8,128)(2,1)} %dy_ref.3) | copy-start | bytes 1572868
  83.9 15.4 %copy-start.38 = (bf16[8,1,64,128]{3,2,1,0:T(8,128)(2,1)}, bf16[8,1,64,128]{3,2,1,0:T(8,128)(2,1)S(1)}, u32[]{:S(2)}) copy-start(bf16[8,1,64,128]{3,2,1,0:T(8,128)(2,1)S(1)} %get-tuple-element.361) | copy-start | bytes 393220
  83.9 5.3 %collective-permute-start.7 = (bf16[512,128]{1,0:T(8,128)(2,1)S(1)}, bf16[512,128]{1,0:T(8,128)(2,1)S(1)}, u32[]{:S(2)}, u32[]{:S(2)}) collective-permute-start(bf16[512,128]{1,0:T(8,128)(2,1)S(1)} %bitcast.133), channel_id=1, source_target_pairs={{0,1},{1,0},{2,3},{3,2},{4,5},{5,4},{6,7},{7,6},{8,9},{9,8},{10,11... | collective-permute-start | bytes 393224 | tf_op jit(solution)/shard_map/ppermute | solution.py:245
  85.6 21.2 %copy-start.2 = (bf16[1024,2048]{1,0:T(8,128)(2,1)S(1)}, bf16[1024,2048]{1,0:T(8,128)(2,1)}, u32[]{:S(2)}) copy-start(bf16[1024,2048]{1,0:T(8,128)(2,1)} %wi_ref.1) | copy-start | bytes 12582916
  89.9 17.0 %copy-start.1 = (bf16[2048,1024]{1,0:T(8,128)(2,1)S(1)}, bf16[2048,1024]{1,0:T(8,128)(2,1)}, u32[]{:S(2)}) copy-start(bf16[2048,1024]{1,0:T(8,128)(2,1)} %wo_ref.3) | copy-start | bytes 12582916
  99.3 7.5 %collective-permute-start.9 = (bf16[128,1024]{1,0:T(8,128)(2,1)}, bf16[128,1024]{1,0:T(8,128)(2,1)S(1)}, u32[]{:S(2)}, u32[]{:S(2)}) collective-permute-start(bf16[128,1024]{1,0:T(8,128)(2,1)} %get-tuple-element.159.h_own), channel_id=1, source_target_pairs={{0,1},{1,0},{2,3},{3,2},{4,5},{5,4},{6,7},{7,6},{8,9},{9,8},{10,11... | collective-permute-start | bytes 786440 | tf_op jit(solution)/shard_map/ppermute | solution.py:245
  124.6 6.4 %collective-permute-start.10 = (bf16[128,1024]{1,0:T(8,128)(2,1)S(1)}, bf16[128,1024]{1,0:T(8,128)(2,1)S(1)}, u32[]{:S(2)}, u32[]{:S(2)}) collective-permute-start(bf16[128,1024]{1,0:T(8,128)(2,1)S(1)} %copy-done.25), channel_id=1, source_target_pairs={{0,1},{1,0},{2,3},{3,2},{4,5},{5,4},{6,7},{7,6},{8,9},{9,8},{10,11... | collective-permute-start | bytes 786440 | tf_op jit(solution)/shard_map/ppermute | solution.py:245
  143.6 15.1 %copy-start.43 = (bf16[128,1024]{1,0:T(8,128)(2,1)S(1)}, bf16[128,1024]{1,0:T(8,128)(2,1)}, u32[]{:S(2)}) copy-start(bf16[128,1024]{1,0:T(8,128)(2,1)} %get-tuple-element.184.refs_2_) | copy-start | bytes 786436
  143.6 15.6 %copy-start.44 = (bf16[128,1024]{1,0:T(8,128)(2,1)S(1)}, bf16[128,1024]{1,0:T(8,128)(2,1)}, u32[]{:S(2)}) copy-start(bf16[128,1024]{1,0:T(8,128)(2,1)} %get-tuple-element.185.refs_6_) | copy-start | bytes 786436
  143.6 5.2 %collective-permute-start.11 = (bf16[512,128]{1,0:T(8,128)(2,1)}, bf16[512,128]{1,0:T(8,128)(2,1)S(1)}, u32[]{:S(2)}, u32[]{:S(2)}) collective-permute-start(bf16[512,128]{1,0:T(8,128)(2,1)} %get-tuple-element.173), channel_id=1, source_target_pairs={{0,1},{1,0},{2,3},{3,2},{4,5},{5,4},{6,7},{7,6},{8,9},{9,8},{10,11... | collective-permute-start | bytes 393224 | tf_op jit(solution)/shard_map/ppermute | solution.py:245
  150.5 20.6 %all-to-all-start.2 = ((bf16[16,1,64,128]{3,2,1,0:T(8,128)(2,1)}), bf16[16,1,64,128]{3,2,1,0:T(8,128)(2,1)S(1)}, u32[]{:S(2)}, u32[]{:S(2)}) async-start(bf16[16,1,64,128]{3,2,1,0:T(8,128)(2,1)} %bitcast.36), calls=%async_computation.2 | async-start | bytes 524288 | tf_op jit(solution)/shard_map/all_to_all | solution.py:1234
  156.6 14.6 %collective-permute-start.17 = (bf16[512,128]{1,0:T(8,128)(2,1)}, bf16[512,128]{1,0:T(8,128)(2,1)}, u32[]{:S(2)}, u32[]{:S(2)}) collective-permute-start(bf16[512,128]{1,0:T(8,128)(2,1)} %get-tuple-element.186), channel_id=1, source_target_pairs={{0,1},{1,0},{2,3},{3,2},{4,5},{5,4},{6,7},{7,6},{8,9},{9,8},{10,11... | collective-permute-start | bytes 393224 | tf_op jit(solution)/shard_map/ppermute | solution.py:245
  157.2 14.0 %collective-permute-start.18 = (bf16[512,128]{1,0:T(8,128)(2,1)}, bf16[512,128]{1,0:T(8,128)(2,1)}, u32[]{:S(2)}, u32[]{:S(2)}) collective-permute-start(bf16[512,128]{1,0:T(8,128)(2,1)} %get-tuple-element.187), channel_id=1, source_target_pairs={{0,1},{1,0},{2,3},{3,2},{4,5},{5,4},{6,7},{7,6},{8,9},{9,8},{10,11... | collective-permute-start | bytes 393224 | tf_op jit(solution)/shard_map/ppermute | solution.py:245
  158.7 12.9 %collective-permute-start.15 = (bf16[128,1024]{1,0:T(8,128)(2,1)S(1)}, bf16[128,1024]{1,0:T(8,128)(2,1)S(1)}, u32[]{:S(2)}, u32[]{:S(2)}) collective-permute-start(bf16[128,1024]{1,0:T(8,128)(2,1)S(1)} %copy-done.43), channel_id=1, source_target_pairs={{0,1},{1,0},{2,3},{3,2},{4,5},{5,4},{6,7},{7,6},{8,9},{9,8},{10,11... | collective-permute-start | bytes 786440 | tf_op jit(solution)/shard_map/ppermute | solution.py:245
  159.2 17.7 %collective-permute-start.16 = (bf16[128,1024]{1,0:T(8,128)(2,1)S(1)}, bf16[128,1024]{1,0:T(8,128)(2,1)}, u32[]{:S(2)}, u32[]{:S(2)}) collective-permute-start(bf16[128,1024]{1,0:T(8,128)(2,1)S(1)} %copy-done.44), channel_id=1, source_target_pairs={{0,1},{1,0},{2,3},{3,2},{4,5},{5,4},{6,7},{7,6},{8,9},{9,8},{10,11... | collective-permute-start | bytes 786440 | tf_op jit(solution)/shard_map/ppermute | solution.py:245
  196.1 2.0 collective-permute-start.19
  202.4 31.4 %all-to-all-start.3 = ((bf16[16,3,64,128]{3,2,1,0:T(8,128)(2,1)}), bf16[16,3,64,128]{3,2,1,0:T(8,128)(2,1)S(1)}, u32[]{:S(2)}, u32[]{:S(2)}) async-start(bf16[16,3,64,128]{3,2,1,0:T(8,128)(2,1)} %combine.1), calls=%async_computation.3 | async-start | bytes 1572864 | tf_op jit(solution)/shard_map/all_to_all | solution.py:1162
  208.1 182.6 %all-gather.4.cloned.1.call-start = ((), (), s32[]{:S(2)}) async-start(), calls=%async_computation.6 | async-start | bytes 8912896 | tf_op jit(solution)/shard_map/all_gather | solution.py:1270
  208.2 9.4 %collective-permute-start.12 = (bf16[2,512,128]{2,1,0:T(8,128)(2,1)}, bf16[2,512,128]{2,1,0:T(8,128)(2,1)S(1)}, u32[]{:S(2)}, u32[]{:S(2)}) collective-permute-start(bf16[2,512,128]{2,1,0:T(8,128)(2,1)} %get-tuple-element.174), channel_id=1, source_target_pairs={{0,1},{1,0},{2,3},{3,2},{4,5},{5,4},{6,7},{7,6},{8,9},{9,8},{10,11... | collective-permute-start | bytes 786440 | tf_op jit(solution)/shard_map/ppermute | solution.py:245
  208.8 14.4 %collective-permute-start.13 = (bf16[128,1024]{1,0:T(8,128)(2,1)S(1)}, bf16[128,1024]{1,0:T(8,128)(2,1)S(1)}, u32[]{:S(2)}, u32[]{:S(2)}) collective-permute-start(bf16[128,1024]{1,0:T(8,128)(2,1)S(1)} %copy-done.42), channel_id=1, source_target_pairs={{0,1},{1,0},{2,3},{3,2},{4,5},{5,4},{6,7},{7,6},{8,9},{9,8},{10,11... | collective-permute-start | bytes 786440 | tf_op jit(solution)/shard_map/ppermute | solution.py:245
  210.3 18.1 %collective-permute-start.14 = (bf16[128,1024]{1,0:T(8,128)(2,1)}, bf16[128,1024]{1,0:T(8,128)(2,1)S(1)}, u32[]{:S(2)}, u32[]{:S(2)}) collective-permute-start(bf16[128,1024]{1,0:T(8,128)(2,1)} %get-tuple-element.176), channel_id=1, source_target_pairs={{0,1},{1,0},{2,3},{3,2},{4,5},{5,4},{6,7},{7,6},{8,9},{9,8},{10,11... | collective-permute-start | bytes 786440 | tf_op jit(solution)/shard_map/ppermute | solution.py:245
  234.6 13.2 %copy-start.28 = (bf16[128,1024]{1,0:T(8,128)(2,1)S(1)}, bf16[128,1024]{1,0:T(8,128)(2,1)}, u32[]{:S(2)}) copy-start(bf16[128,1024]{1,0:T(8,128)(2,1)} %get-tuple-element.344.x_ref) | copy-start | bytes 786436
  234.7 13.5 %copy-start.33 = (f32[2,512,128]{2,1,0:T(8,128)S(1)}, f32[2,512,128]{2,1,0:T(8,128)}, u32[]{:S(2)}) copy-start(f32[2,512,128]{2,1,0:T(8,128)} %get-tuple-element.206) | copy-start | bytes 1572868
  234.7 13.7 %copy-start.32 = (f32[128,1024]{1,0:T(8,128)S(1)}, f32[128,1024]{1,0:T(8,128)}, u32[]{:S(2)}) copy-start(f32[128,1024]{1,0:T(8,128)} %get-tuple-element.158.x2_ref) | copy-start | bytes 1572868
  247.0 190.9 %all-gather.6.cloned.1.call-start = ((), (), s32[]{:S(2)}) async-start(), calls=%async_computation.7 | async-start | bytes 6684672 | tf_op jit(solution)/shard_map/all_gather | solution.py:1295
  247.3 16.5 %collective-permute-start.20 = (bf16[256,3072]{1,0:T(8,128)(2,1)}, bf16[256,3072]{1,0:T(8,128)(2,1)}, u32[]{:S(2)}, u32[]{:S(2)}) collective-permute-start(bf16[256,3072]{1,0:T(8,128)(2,1)} %get-tuple-element.200), channel_id=1, source_target_pairs={{0,2},{2,0},{4,6},{6,4},{8,10},{10,8},{12,14},{14,12},{16,18},{18,... | collective-permute-start | bytes 4718600 | tf_op jit(solution)/shard_map/ppermute | solution.py:249
  247.5 16.3 %collective-permute-start.21 = (bf16[512,1536]{1,0:T(8,128)(2,1)}, bf16[512,1536]{1,0:T(8,128)(2,1)}, u32[]{:S(2)}, u32[]{:S(2)}) collective-permute-start(bf16[512,1536]{1,0:T(8,128)(2,1)} %get-tuple-element.205), channel_id=1, source_target_pairs={{0,2},{2,0},{4,6},{6,4},{8,10},{10,8},{12,14},{14,12},{16,18},{18,... | collective-permute-start | bytes 4718600 | tf_op jit(solution)/shard_map/ppermute | solution.py:249
  248.2 7.5 %collective-permute-start.22 = (bf16[2,512,128]{2,1,0:T(8,128)(2,1)S(1)}, bf16[2,512,128]{2,1,0:T(8,128)(2,1)S(1)}, u32[]{:S(2)}, u32[]{:S(2)}) collective-permute-start(bf16[2,512,128]{2,1,0:T(8,128)(2,1)S(1)} %fusion.15), channel_id=1, source_target_pairs={{0,2},{2,0},{4,6},{6,4},{8,10},{10,8},{12,14},{14,12},{16,18},{18,... | collective-permute-start | bytes 786440 | tf_op jit(solution)/shard_map/ppermute | solution.py:249
  249.5 9.2 %collective-permute-start.24 = (bf16[128,1024]{1,0:T(8,128)(2,1)S(1)}, bf16[128,1024]{1,0:T(8,128)(2,1)S(1)}, u32[]{:S(2)}, u32[]{:S(2)}) collective-permute-start(bf16[128,1024]{1,0:T(8,128)(2,1)S(1)} %add_convert_fusion.1), channel_id=1, source_target_pairs={{0,1},{1,0},{2,3},{3,2},{4,5},{5,4},{6,7},{7,6},{8,9},{9,8},{10,11... | collective-permute-start | bytes 786440 | tf_op jit(solution)/shard_map/ppermute | solution.py:245
  254.1 9.7 %collective-permute-start.23 = (bf16[128,1024]{1,0:T(8,128)(2,1)}, bf16[128,1024]{1,0:T(8,128)(2,1)S(1)}, u32[]{:S(2)}, u32[]{:S(2)}) collective-permute-start(bf16[128,1024]{1,0:T(8,128)(2,1)} %get-tuple-element.208), channel_id=1, source_target_pairs={{0,1},{1,0},{2,3},{3,2},{4,5},{5,4},{6,7},{7,6},{8,9},{9,8},{10,11... | collective-permute-start | bytes 786440 | tf_op jit(solution)/shard_map/ppermute | solution.py:245
  270.0 36.0 %collective-permute-start.25 = (bf16[128,3072]{1,0:T(8,128)(2,1)}, bf16[128,3072]{1,0:T(8,128)(2,1)S(1)}, u32[]{:S(2)}, u32[]{:S(2)}) collective-permute-start(bf16[128,3072]{1,0:T(8,128)(2,1)} %get-tuple-element.217), channel_id=1, source_target_pairs={{0,4},{2,6},{4,0},{6,2},{8,12},{10,14},{12,8},{14,10},{16,20},{18,... | collective-permute-start | bytes 2359304 | tf_op jit(solution)/shard_map/ppermute | solution.py:249
  271.6 37.0 %collective-permute-start.26 = (bf16[256,1536]{1,0:T(8,128)(2,1)}, bf16[256,1536]{1,0:T(8,128)(2,1)S(1)}, u32[]{:S(2)}, u32[]{:S(2)}) collective-permute-start(bf16[256,1536]{1,0:T(8,128)(2,1)} %get-tuple-element.218), channel_id=1, source_target_pairs={{0,8},{2,10},{4,12},{6,14},{8,0},{10,2},{12,4},{14,6},{16,24},{18,... | collective-permute-start | bytes 2359304 | tf_op jit(solution)/shard_map/ppermute | solution.py:249
  275.3 7.7 %collective-permute-start.28 = (bf16[128,1024]{1,0:T(8,128)(2,1)S(1)}, bf16[128,1024]{1,0:T(8,128)(2,1)S(1)}, u32[]{:S(2)}, u32[]{:S(2)}) collective-permute-start(bf16[128,1024]{1,0:T(8,128)(2,1)S(1)} %fusion.12), channel_id=1, source_target_pairs={{0,1},{1,0},{2,3},{3,2},{4,5},{5,4},{6,7},{7,6},{8,9},{9,8},{10,11... | collective-permute-start | bytes 786440 | tf_op jit(solution)/shard_map/ppermute | solution.py:245
  275.8 30.3 %collective-permute-start.27 = (bf16[2,512,128]{2,1,0:T(8,128)(2,1)S(1)}, bf16[2,512,128]{2,1,0:T(8,128)(2,1)S(1)}, u32[]{:S(2)}, u32[]{:S(2)}) collective-permute-start(bf16[2,512,128]{2,1,0:T(8,128)(2,1)S(1)} %get-tuple-element.345), channel_id=1, source_target_pairs={{0,4},{2,6},{4,0},{6,2},{8,12},{10,14},{12,8},{14,10},{16,20},{18,... | collective-permute-start | bytes 786440 | tf_op jit(solution)/shard_map/ppermute | solution.py:249
  276.0 7.1 %collective-permute-start.29 = (f32[6,1024]{1,0:T(8,128)S(1)}, f32[6,1024]{1,0:T(8,128)S(1)}, u32[]{:S(2)}, u32[]{:S(2)}) collective-permute-start(f32[6,1024]{1,0:T(8,128)S(1)} %pad_maximum_fusion.5), channel_id=1, source_target_pairs={{0,1},{1,0},{2,3},{3,2},{4,5},{5,4},{6,7},{7,6},{8,9},{9,8},{10,11... | collective-permute-start | bytes 73736 | tf_op jit(solution)/shard_map/ppermute | solution.py:245
  283.0 36.7 %copy-start.49 = (bf16[128,1024]{1,0:T(8,128)(2,1)}, bf16[128,1024]{1,0:T(8,128)(2,1)S(1)}, u32[]{:S(2)}) copy-start(bf16[128,1024]{1,0:T(8,128)(2,1)S(1)} %collective-permute-done.28) | copy-start | bytes 786436
  314.3 27.8 %collective-permute-start.30 = (bf16[64,3072]{1,0:T(8,128)(2,1)}, bf16[64,3072]{1,0:T(8,128)(2,1)S(1)}, u32[]{:S(2)}, u32[]{:S(2)}) collective-permute-start(bf16[64,3072]{1,0:T(8,128)(2,1)} %get-tuple-element.227), channel_id=1, source_target_pairs={{0,8},{2,10},{4,12},{6,14},{8,0},{10,2},{12,4},{14,6},{16,24},{18,... | collective-permute-start | bytes 1179656 | tf_op jit(solution)/shard_map/ppermute | solution.py:249
  316.3 25.8 %collective-permute-start.31 = (bf16[128,1536]{1,0:T(8,128)(2,1)}, bf16[128,1536]{1,0:T(8,128)(2,1)S(1)}, u32[]{:S(2)}, u32[]{:S(2)}) collective-permute-start(bf16[128,1536]{1,0:T(8,128)(2,1)} %get-tuple-element.228), channel_id=1, source_target_pairs={{0,4},{2,6},{4,0},{6,2},{8,12},{10,14},{12,8},{14,10},{16,20},{18,... | collective-permute-start | bytes 1179656 | tf_op jit(solution)/shard_map/ppermute | solution.py:249
  319.6 22.5 %collective-permute-start.32 = (bf16[2,512,128]{2,1,0:T(8,128)(2,1)}, bf16[2,512,128]{2,1,0:T(8,128)(2,1)S(1)}, u32[]{:S(2)}, u32[]{:S(2)}) collective-permute-start(bf16[2,512,128]{2,1,0:T(8,128)(2,1)} %fusion.16), channel_id=1, source_target_pairs={{0,8},{2,10},{4,12},{6,14},{8,0},{10,2},{12,4},{14,6},{16,24},{18,... | collective-permute-start | bytes 786440 | tf_op jit(solution)/shard_map/ppermute | solution.py:249
  319.7 1.3 collective-permute-start.33
  342.3 28.8 %collective-permute-start.36 = (bf16[2,512,128]{2,1,0:T(8,128)(2,1)S(1)}, bf16[2,512,128]{2,1,0:T(8,128)(2,1)S(1)}, u32[]{:S(2)}, u32[]{:S(2)}) collective-permute-start(bf16[2,512,128]{2,1,0:T(8,128)(2,1)S(1)} %fusion.20), channel_id=1, source_target_pairs={{0,16},{2,18},{4,20},{6,22},{8,24},{10,26},{12,28},{14,30},{16,0},... | collective-permute-start | bytes 786440 | tf_op jit(solution)/shard_map/ppermute | solution.py:249
  349.1 26.7 %copy-start.50 = (bf16[128,1024]{1,0:T(8,128)(2,1)S(1)}, bf16[128,1024]{1,0:T(8,128)(2,1)}, u32[]{:S(2)}) copy-start(bf16[128,1024]{1,0:T(8,128)(2,1)} %copy-done.49) | copy-start | bytes 786436
  349.1 18.6 %collective-permute-start.34 = (bf16[32,3072]{1,0:T(8,128)(2,1)}, bf16[32,3072]{1,0:T(8,128)(2,1)S(1)}, u32[]{:S(2)}, u32[]{:S(2)}) collective-permute-start(bf16[32,3072]{1,0:T(8,128)(2,1)} %get-tuple-element.235), channel_id=1, source_target_pairs={{0,16},{2,18},{4,20},{6,22},{8,24},{10,26},{12,28},{14,30},{16,0},... | collective-permute-start | bytes 589832 | tf_op jit(solution)/shard_map/ppermute | solution.py:249
  349.8 21.3 %collective-permute-start.35 = (bf16[64,1536]{1,0:T(8,128)(2,1)}, bf16[64,1536]{1,0:T(8,128)(2,1)S(1)}, u32[]{:S(2)}, u32[]{:S(2)}) collective-permute-start(bf16[64,1536]{1,0:T(8,128)(2,1)} %get-tuple-element.236), channel_id=1, source_target_pairs={{0,16},{2,18},{4,20},{6,22},{8,24},{10,26},{12,28},{14,30},{16,0},... | collective-permute-start | bytes 589832 | tf_op jit(solution)/shard_map/ppermute | solution.py:249
  352.1 3.9 collective-permute-start.37
  376.7 6.1 %collective-permute-start.39 = (f32[6,1024]{1,0:T(8,128)S(1)}, f32[6,1024]{1,0:T(8,128)S(1)}, u32[]{:S(2)}, u32[]{:S(2)}) collective-permute-start(f32[6,1024]{1,0:T(8,128)S(1)} %add.320), channel_id=1, source_target_pairs={{0,8},{2,10},{4,12},{6,14},{8,0},{10,2},{12,4},{14,6},{16,24},{18,... | collective-permute-start | bytes 73736 | tf_op jit(solution)/shard_map/ppermute | solution.py:249
  378.6 11.3 %collective-permute-start.38 = (bf16[128,1024]{1,0:T(8,128)(2,1)S(1)}, bf16[128,1024]{1,0:T(8,128)(2,1)S(1)}, u32[]{:S(2)}, u32[]{:S(2)}) collective-permute-start(bf16[128,1024]{1,0:T(8,128)(2,1)S(1)} %fusion), channel_id=1, source_target_pairs={{0,1},{1,0},{2,3},{3,2},{4,5},{5,4},{6,7},{7,6},{8,9},{9,8},{10,11... | collective-permute-start | bytes 786440 | tf_op jit(solution)/shard_map/ppermute | solution.py:245
  382.9 6.4 %collective-permute-start.40 = (f32[6,1024]{1,0:T(8,128)S(1)}, f32[6,1024]{1,0:T(8,128)S(1)}, u32[]{:S(2)}, u32[]{:S(2)}) collective-permute-start(f32[6,1024]{1,0:T(8,128)S(1)} %add.321), channel_id=1, source_target_pairs={{0,16},{2,18},{4,20},{6,22},{8,24},{10,26},{12,28},{14,30},{16,0},... | collective-permute-start | bytes 73736 | tf_op jit(solution)/shard_map/ppermute | solution.py:249
  395.5 42.5 %copy-start.23 = (s32[2,16]{1,0:T(2,128)S(1)}, s32[2,16]{1,0:T(2,128)}, u32[]{:S(2)}) copy-start(s32[2,16]{1,0:T(2,128)} %constant.159.clone.devices) | copy-start | bytes 388
  (44 other events, 211.8 us)
Sparse Core Ops, SparseCore 0:
  123.8 123.1 reduce-scatter.1
  249.1 92.8 all-gather.3
  374.1 63.7 all-gather.5
where the time goes:
time: 461 us; the launch traced here: 453 us
  waiting for transfers between devices  183 us (40%)
  Pallas kernels  128 us (28%)
  starting transfers between devices  72.2 us (16%)
  local copies, waits for them, and re-layouts  36.3 us (8%)
  between operations  14.9 us (3%)
  other arithmetic  13.2 us (3%)
  matrix products  5.31 us (1%)
    pallas_call x18, Pallas kernels, run(): call(*[pltpu.with_memory_space_constraint(a, pltpu.HBM) if a.size >= leas...  128 us
    ppermute x21, waiting for transfers between devices, over_blk(): lax.ppermute(value, 'blk', [(i, i ^ bit) for i in range(lax.axis_size('bl...  70.6 us
    ppermute x20, waiting for transfers between devices, over_x(): return lax.ppermute(value, 'tp', SWAP)  52 us
    all_gather x1, waiting for transfers between devices, shards(): pieces = lax.all_gather(last_halves(heads, pairs), 'blk')  31.8 us
    ppermute x20, starting transfers between devices, over_x(): return lax.ppermute(value, 'tp', SWAP)  26.4 us
    ppermute x21, starting transfers between devices, over_blk(): lax.ppermute(value, 'blk', [(i, i ^ bit) for i in range(lax.axis_size('bl...  20.4 us
    unnamed x122, local copies, waits for them, and re-layouts  20.3 us
    all_to_all x2, starting transfers between devices, bring_heads(): got = lax.all_to_all(array, 'blk', 0, 0, tiled=True)  11.2 us
  transfers between devices with their start and end apart: 48, of which 28 were waited for; matrix products, arithmetic and copies ran while one was open for 8% of the time, Pallas kernels for 20%

commit v1 on v0

--- a/solution.py
+++ b/solution.py
@@ -1233,11 +1233,11 @@
     sent = jnp.concatenate([low, high], axis=1).reshape(blk_count, 1, HEAD_DIM, sub)
     grads = lax.all_to_all(sent, "blk", 0, 0, tiled=True)[:, 0]
     grads = grads.transpose(1, 0, 2).reshape(HEAD_DIM, blk_count * sub)
-    dx1_other, dx2_other, dqc_other, c_other = [
-        over_x(value) for value in after((dx1_low, dx2_low, dqc_sent, c_sent), da_other)
+    dx1_other, dqc_other, c_other = [
+        over_x(value) for value in after((dx1_low, dqc_sent, c_sent), da_other)
     ]
-    grads, dx1_other, dx2_other, dqc_other, c_other = lax.optimization_barrier(
-        (grads, dx1_other, dx2_other, dqc_other, c_other)
+    grads, dx1_other, dqc_other, c_other = lax.optimization_barrier(
+        (grads, dx1_other, dqc_other, c_other)
     )
     dq, parts = attend_back(
         queries, keys, values, rows_all, first, flip, out, log_total, grads, sub
@@ -1248,8 +1248,8 @@
     parts_got = over_blk(parts[1], 1)
     sent = combine(dq, parts, parts_got, scale)
     back = bring_heads(sent)
-    text_got, h2_other, y_got = after(
-        [over_x(value) for value in after((text_sent, h2_own, y_sent), da_other)], sent
+    text_got, h2_other, y_got, dx2_other = after(
+        [over_x(value) for value in after((text_sent, h2_own, y_sent, dx2_low), da_other)], sent
     )
     text_part = text_own + text_got.astype(F32)
     pair_send, pair_keep = pair_grads(

time: 461 us -> 457 us (level)
  starting transfers between devices: 72.2 us -> 66.6 us
    reduce_scatter x1, waiting for transfers between devices: 7.21 us -> 1.54 us  [shards(): lax.psum_scatter(hidden_both, 'blk', scatter_dimension=0, tiled=True)]
    unnamed x122 -> x128, local copies, waits for them, and re-layouts: 20.3 us -> 22.4 us
  transfers between devices with their start and end apart: 48 -> 48, of which waited for: 28 -> 27; matrix products, arithmetic and copies ran while one was open for 8% -> 9% of each run, Pallas kernels for 20% -> 21%
where the time goes in v1:
time: 457 us; the launch traced here: 448 us
  waiting for transfers between devices  181 us (40%)
  Pallas kernels  128 us (28%)
  starting transfers between devices  66.6 us (15%)
  local copies, waits for them, and re-layouts  38.3 us (8%)
  between operations  14.9 us (3%)
  other arithmetic  13.2 us (3%)
  matrix products  5.31 us (1%)
    pallas_call x18, Pallas kernels, run(): call(*[pltpu.with_memory_space_constraint(a, pltpu.HBM) if a.size >= leas...  128 us
    ppermute x21, waiting for transfers between devices, over_blk(): lax.ppermute(value, 'blk', [(i, i ^ bit) for i in range(lax.axis_size('bl...  73.2 us
    ppermute x20, waiting for transfers between devices, over_x(): return lax.ppermute(value, 'tp', SWAP)  51.2 us
    all_gather x1, waiting for transfers between devices, shards(): pieces = lax.all_gather(last_halves(heads, pairs), 'blk')  33.2 us
    ppermute x20, starting transfers between devices, over_x(): return lax.ppermute(value, 'tp', SWAP)  23.7 us
    unnamed x128, local copies, waits for them, and re-layouts  22.4 us
    ppermute x21, starting transfers between devices, over_blk(): lax.ppermute(value, 'blk', [(i, i ^ bit) for i in range(lax.axis_size('bl...  17.6 us
    all_to_all x1, waiting for transfers between devices, shards(): grads = lax.all_to_all(sent, 'blk', 0, 0, tiled=True)[:, 0]  11.9 us
  transfers between devices with their start and end apart: 48, of which 27 were waited for; matrix products, arithmetic and copies ran while one was open for 9% of the time, Pallas kernels for 21%

profile of v1, /device:TPU:0, one launch (start us, length us, event | category | flops | bytes accessed | tf_op | source)
XLA Modules:
  0.0 448.0 jit_solution(3192241828434920255)
XLA Ops:
  13.4 2.2 embed.1
  16.4 7.6 %all-to-all-start = ((bf16[16,3,64,128]{3,2,1,0:T(8,128)(2,1)}), bf16[16,3,64,128]{3,2,1,0:T(8,128)(2,1)}, u32[]{:S(2)}, u32[]{:S(2)}) async-start(bf16[16,3,64,128]{3,2,1,0:T(8,128)(2,1)} %get-tuple-element.139), calls=%async_computation | async-start | bytes 1572864 | tf_op jit(solution)/shard_map/all_to_all | solution.py:1165
  24.0 1.9 constant_dynamic-slice_fusion.4
  32.9 9.9 %all-to-all-done = bf16[16,3,64,128]{3,2,1,0:T(8,128)(2,1)} async-done(((bf16[16,3,64,128]{3,2,1,0:T(8,128)(2,1)}), bf16[16,3,64,128]{3,2,1,0:T(8,128)(2,1)}, u32[]{:S(2)}, u32[]{:S(2)}) %all-to-all-start) | async-done | bytes 786464 | tf_op jit(solution)/shard_map/all_to_all | solution.py:1165
  47.7 1.6 copy.139
  49.7 15.3 %attend.1 = (f32[64,2048]{1,0:T(8,128)S(1)}, f32[1,2048]{1,0:T(1,128)S(1)}) custom-call(s32[4,4]{1,0:T(4,128)S(1)} %pad_add_fusion.ranges, s32[1]{0:T(128)} %bitcast.7.flips, bf16[64,2048]{1,0:T(8,128)(2,1)S(1)} %copy_bitcast_fusion.2.q_ref, bf16[64,4096]{1,0:T(8,128)(2,1)S(1)} %squeeze.53.k_ref, bf16[64,4096]{1,0:T(8,128)(2,1)S(1)} %squeeze.54.v_ref, ...), custom_call_target="tpu_custom_call" | custom-call | bytes 55500000 | tf_op jit(solution)/shard_map/attend/pallas_call | solution.py:29
  66.6 5.5 %all-to-all-start.1 = ((bf16[16,1,64,128]{3,2,1,0:T(8,128)(2,1)}), bf16[16,1,64,128]{3,2,1,0:T(8,128)(2,1)}, u32[]{:S(2)}, u32[]{:S(2)}) async-start(bf16[16,1,64,128]{3,2,1,0:T(8,128)(2,1)} %bitcast_bitcast_fusion), calls=%async_computation.1 | async-start | bytes 524288 | tf_op jit(solution)/shard_map/all_to_all | solution.py:1162
  73.3 1.7 fusion.2
  75.7 1.5 collective-permute-start.8
  78.0 3.7 weld.1
  82.2 1.7 constant_dynamic-slice_fusion.2
  83.9 1.5 collective-permute-start.7
  85.6 2.0 fusion.19
  87.6 1.6 collective-permute-done.7.a_other
  89.8 9.4 %cross_forward.1 = (f32[128,1024]{1,0:T(8,128)}, f32[128,1024]{1,0:T(8,128)}, bf16[128,1024]{1,0:T(8,128)(2,1)}, bf16[128,1024]{1,0:T(8,128)(2,1)}, bf16[2,512,1...) custom-call(bf16[512,128]{1,0:T(8,128)(2,1)} %bitcast.131, ...), custom_call_target="tpu_custom_call" | custom-call | bytes 25900000 | tf_op jit(solution)/shard_map/cross_forward/pallas_call | solution.py:29
  99.3 1.6 collective-permute-start.9
  100.9 5.9 %collective-permute-done.9.h_other = bf16[128,1024]{1,0:T(8,128)(2,1)S(1)} collective-permute-done((bf16[128,1024]{1,0:T(8,128)(2,1)}, bf16[128,1024]{1,0:T(8,128)(2,1)S(1)}, u32[]{:S(2)}, u32[]{:S(2)}) %collective-permute-start.9) | collective-permute-done | bytes 262176 | tf_op jit(solution)/shard_map/ppermute | solution.py:245
  107.7 8.4 %hidden_pass.1 = (bf16[256,2048]{1,0:T(8,128)(2,1)S(1)}, bf16[256,2048]{1,0:T(8,128)(2,1)S(1)}, f32[128,1024]{1,0:T(8,128)S(1)}, bf16[128,1024]{1,0:T(8,128)(2,1)S(1)}) custom-call(s32[1]{0:T(128)} %bitcast.33.tp_ref.place.tp, bf16[128,1024]{1,0:T(8,128)(2,1)S(1)} %copy-done.12, bf16[128,1024]{1,0:T(8,128)(2,1)S(1)} %collective-permute-done.9.h_other, ...), custom_call_target="tpu_custom_call" | custom-call | bytes 37000000 | tf_op jit(solution)/shard_map/hidden_pass/pallas_call | solution.py:29
  116.2 7.4 %hidden_grads.1 = (bf16[2048,2048]{1,0:T(8,128)(2,1)}, f32[128,1024]{1,0:T(8,128)}, bf16[128,1024]{1,0:T(8,128)(2,1)}) custom-call(s32[1]{0:T(128)} %bitcast.33.tp_ref.place.tp, bf16[128,1024]{1,0:T(8,128)(2,1)S(1)} %copy-done.12, bf16[128,1024]{1,0:T(8,128)(2,1)S(1)} %collective-permute-done.9.h_other, bf16[256,1024]{1,0:T(8,128)(2,1)S(1)} %copy-done.6, ...), custom_call_target="tpu_custom_call" | custom-call | bytes 33300000 | tf_op jit(solution)/shard_map/hidden_grads/pallas_call | solution.py:29
  124.6 1.5 collective-permute-start.10
  126.8 4.2 collective-permute-done.10.dh_got
  131.7 11.9 %cross_backward.1 = (f32[128,1024]{1,0:T(8,128)}, bf16[128,1024]{1,0:T(8,128)(2,1)}, bf16[128,1024]{1,0:T(8,128)(2,1)}, bf16[512,128]{1,0:T(8,128)(2,1)}, bf16[5...) custom-call(f32[128,1024]{1,0:T(8,128)} %copy-done.14, ...), custom_call_target="tpu_custom_call" | custom-call | bytes 33300000 | tf_op jit(solution)/shard_map/cross_backward/pallas_call | solution.py:29
  143.6 1.5 collective-permute-start.11
  145.1 3.7 collective-permute-done.11
  150.5 6.0 %all-to-all-start.2 = ((bf16[16,1,64,128]{3,2,1,0:T(8,128)(2,1)}), bf16[16,1,64,128]{3,2,1,0:T(8,128)(2,1)S(1)}, u32[]{:S(2)}, u32[]{:S(2)}) async-start(bf16[16,1,64,128]{3,2,1,0:T(8,128)(2,1)} %bitcast.36), calls=%async_computation.2 | async-start | bytes 524288 | tf_op jit(solution)/shard_map/all_to_all | solution.py:1234
  159.2 11.9 %all-to-all-done.2 = bf16[16,1,64,128]{3,2,1,0:T(8,128)(2,1)S(1)} async-done(((bf16[16,1,64,128]{3,2,1,0:T(8,128)(2,1)}), bf16[16,1,64,128]{3,2,1,0:T(8,128)(2,1)S(1)}, u32[]{:S(2)}, u32[]{:S(2)}) %all-to-all-start.2) | async-done | bytes 262176 | tf_op jit(solution)/shard_map/all_to_all | solution.py:1234
  173.6 17.4 %attend_back.1 = (bf16[16,64,128]{2,1,0:T(8,128)(2,1)S(1)}, bf16[2,16,2,64,128]{4,3,2,1,0:T(8,128)(2,1)S(1)}) custom-call(s32[4,4]{1,0:T(4,128)S(1)} %pad_add_fusion.ranges, s32[1]{0:T(128)} %bitcast.7.flips, bf16[64,2048]{1,0:T(8,128)(2,1)S(1)} %copy_bitcast_fusion.2.q_ref, bf16[64,4096]{1,0:T(8,128)(2,1)S(1)} %squeeze.53.k_ref, ...), custom_call_target="tpu_custom_call" | custom-call | bytes 62900000 | tf_op jit(solution)/shard_map/attend_back/pallas_call | solution.py:29
  191.8 1.9 collective-permute-done.19.got_ref
  194.4 3.5 combine.1
  198.0 5.7 %all-to-all-start.3 = ((bf16[16,3,64,128]{3,2,1,0:T(8,128)(2,1)}), bf16[16,3,64,128]{3,2,1,0:T(8,128)(2,1)S(1)}, u32[]{:S(2)}, u32[]{:S(2)}) async-start(bf16[16,3,64,128]{3,2,1,0:T(8,128)(2,1)} %combine.1), calls=%async_computation.3 | async-start | bytes 1572864 | tf_op jit(solution)/shard_map/all_to_all | solution.py:1162
  207.9 5.3 %collective-permute-done.12 = bf16[2,512,128]{2,1,0:T(8,128)(2,1)S(1)} collective-permute-done((bf16[2,512,128]{2,1,0:T(8,128)(2,1)}, bf16[2,512,128]{2,1,0:T(8,128)(2,1)S(1)}, u32[]{:S(2)}, u32[]{:S(2)}) %collective-permute-start.12) | collective-permute-done | bytes 262176 | tf_op jit(solution)/shard_map/ppermute | solution.py:245
  213.2 5.6 %collective-permute-done.13.refs_11_ = bf16[128,1024]{1,0:T(8,128)(2,1)S(1)} collective-permute-done((bf16[128,1024]{1,0:T(8,128)(2,1)S(1)}, bf16[128,1024]{1,0:T(8,128)(2,1)S(1)}, u32[]{:S(2)}, u32[]{:S(2)}) %collective-permute-start.13) | collective-permute-done | bytes 262176 | tf_op jit(solution)/shard_map/ppermute | solution.py:245
  218.8 5.6 %collective-permute-done.14 = bf16[128,1024]{1,0:T(8,128)(2,1)S(1)} collective-permute-done((bf16[128,1024]{1,0:T(8,128)(2,1)}, bf16[128,1024]{1,0:T(8,128)(2,1)S(1)}, u32[]{:S(2)}, u32[]{:S(2)}) %collective-permute-start.14) | collective-permute-done | bytes 262176 | tf_op jit(solution)/shard_map/ppermute | solution.py:245
  224.4 5.1 %collective-permute-done.15.refs_7_ = bf16[128,1024]{1,0:T(8,128)(2,1)S(1)} collective-permute-done((bf16[128,1024]{1,0:T(8,128)(2,1)S(1)}, bf16[128,1024]{1,0:T(8,128)(2,1)S(1)}, u32[]{:S(2)}, u32[]{:S(2)}) %collective-permute-start.15) | collective-permute-done | bytes 262176 | tf_op jit(solution)/shard_map/ppermute | solution.py:245
  230.2 4.8 %pair_grads.1 = (bf16[256,3072]{1,0:T(8,128)(2,1)}, bf16[256,3072]{1,0:T(8,128)(2,1)}) custom-call(s32[1]{0:T(128)} %bitcast.17.core, bf16[512,128]{1,0:T(8,128)(2,1)} %bitcast.132, bf16[512,128]{1,0:T(8,128)(2,1)} %bitcast.134, bf16[128,1024]{1,0:T(8,128)(2,1)} %get-tuple-element.185.refs_2_, bf16[128,1024]{1,0:T(8,128)(2,1)} %copy-done.45, ...), custom_call_target="tpu_custom_call" | custom-call | bytes 14800000 | tf_op jit(solution)/shard_map/pair_grads/pallas_call | solution.py:29
  237.3 3.7 head_grads.1
  241.0 1.5 reduce-scatter.2.cloned.1.call-done
  245.8 4.0 project_back.1
  251.3 3.0 collective-permute-done.24
  254.3 5.1 %collective-permute-done.23 = bf16[128,1024]{1,0:T(8,128)(2,1)S(1)} collective-permute-done((bf16[128,1024]{1,0:T(8,128)(2,1)}, bf16[128,1024]{1,0:T(8,128)(2,1)S(1)}, u32[]{:S(2)}, u32[]{:S(2)}) %collective-permute-start.23) | collective-permute-done | bytes 262176 | tf_op jit(solution)/shard_map/ppermute | solution.py:245
  259.4 6.2 %fold.3 = (bf16[128,3072]{1,0:T(8,128)(2,1)}, bf16[128,3072]{1,0:T(8,128)(2,1)}, bf16[256,1536]{1,0:T(8,128)(2,1)}, bf16[256,1536]{1,0:T(8,128)(2,1)}) custom-call(s32[2]{0:T(128)S(1)} %get-tuple-element.373.sides, bf16[256,3072]{1,0:T(8,128)(2,1)} %get-tuple-element.213.refs_0_, bf16[256,3072]{1,0:T(8,128)(2,1)} %collective-permute-done.20.refs_1_, ...), custom_call_target="tpu_custom_call" | custom-call | bytes 11100000 | tf_op jit(solution)/shard_map/fold/pallas_call | solution.py:29
  265.6 1.6 collective-permute-start.25
  270.8 5.5 %collective-permute-done.29 = f32[6,1024]{1,0:T(8,128)S(1)} collective-permute-done((f32[6,1024]{1,0:T(8,128)S(1)}, f32[6,1024]{1,0:T(8,128)S(1)}, u32[]{:S(2)}, u32[]{:S(2)}) %collective-permute-start.29) | collective-permute-done | bytes 24608 | tf_op jit(solution)/shard_map/ppermute | solution.py:245
  276.2 23.7 %collective-permute-done.27 = bf16[2,512,128]{2,1,0:T(8,128)(2,1)S(1)} collective-permute-done((bf16[2,512,128]{2,1,0:T(8,128)(2,1)S(1)}, bf16[2,512,128]{2,1,0:T(8,128)(2,1)S(1)}, u32[]{:S(2)}, u32[]{:S(2)}) %collective-permute-start.27) | collective-permute-done | bytes 262176 | tf_op jit(solution)/shard_map/ppermute | solution.py:249
  302.0 4.9 %fold.4 = (bf16[64,3072]{1,0:T(8,128)(2,1)}, bf16[64,3072]{1,0:T(8,128)(2,1)}, bf16[128,1536]{1,0:T(8,128)(2,1)}, bf16[128,1536]{1,0:T(8,128)(2,1)}) custom-call(s32[2]{0:T(128)S(1)} %get-tuple-element.374.sides, bf16[128,3072]{1,0:T(8,128)(2,1)} %get-tuple-element.223.refs_0_, bf16[128,3072]{1,0:T(8,128)(2,1)} %copy-done.35, ...), custom_call_target="tpu_custom_call" | custom-call | bytes 11100000 | tf_op jit(solution)/shard_map/fold/pallas_call | solution.py:29
  306.9 1.6 collective-permute-start.31
  309.3 2.0 collective-permute-start.32
  312.6 23.4 %collective-permute-done.32 = bf16[2,512,128]{2,1,0:T(8,128)(2,1)S(1)} collective-permute-done((bf16[2,512,128]{2,1,0:T(8,128)(2,1)}, bf16[2,512,128]{2,1,0:T(8,128)(2,1)S(1)}, u32[]{:S(2)}, u32[]{:S(2)}) %collective-permute-start.32) | collective-permute-done | bytes 262176 | tf_op jit(solution)/shard_map/ppermute | solution.py:249
  336.1 1.8 collective-permute-start.36
  338.0 4.2 fold.5
  343.4 1.8 collective-permute-start.35
  345.2 1.7 collective-permute-start.37
  346.9 2.3 collective-permute-done.37
  349.1 15.4 %collective-permute-done.34.pair_got = bf16[32,3072]{1,0:T(8,128)(2,1)S(1)} collective-permute-done((bf16[32,3072]{1,0:T(8,128)(2,1)}, bf16[32,3072]{1,0:T(8,128)(2,1)S(1)}, u32[]{:S(2)}, u32[]{:S(2)}) %collective-permute-start.34) | collective-permute-done | bytes 196640 | tf_op jit(solution)/shard_map/ppermute | solution.py:249
  364.5 2.4 collective-permute-done.35.head_got
  367.7 2.1 last_halves.1
  375.2 1.5 collective-permute-start.38
  376.8 2.3 collective-permute-start.40
  379.1 1.7 convolution_bitcast_fusion.1
  384.1 2.9 copy.148
  387.0 1.8 copy.149
  388.8 10.7 %hidden_out.1 = (f32[2048,1024]{1,0:T(8,128)}, f32[1024,2048]{1,0:T(8,128)}) custom-call(bf16[2048,2048]{1,0:T(8,128)(2,1)} %all-gather.4.cloned.1.call-done.both_ref), custom_call_target="tpu_custom_call" | custom-call | bytes 33300000 | tf_op jit(solution)/shard_map/hidden_out/pallas_call | solution.py:29
  399.5 33.2 %all-gather.6.cloned.1.call-done = bf16[2048,1536]{1,0:T(8,128)(2,1)} async-done(((bf16[128,1536]{1,0:T(8,128)(2,1)}), bf16[2048,1536]{1,0:T(8,128)(2,1)}) %all-gather.6.cloned.1.call-update) | async-done | bytes 6291472 | tf_op jit(solution)/shard_map/all_gather | solution.py:1295
  432.7 8.3 %widen.1 = (f32[1024,512]{1,0:T(8,128)}, f32[1024,512]{1,0:T(8,128)}, f32[1024,512]{1,0:T(8,128)}, f32[512,1024]{1,0:T(8,128)}, f32[512,1024]{1,0:T(8,128)}, /*index=5*/f32[1024,512]{1,0:T(8,128)}) custom-call(s32[2,16]{1,0:T(2,128)S(1)} %copy-done.23, bf16[16,128,1536]{2,1,0:T(8,128)(2,1)} %bitcast.121, bf16[16,128,1536]{2,1,0:T(8,128)(2,1)} %bitcast.122, ...), custom_call_target="tpu_custom_call" | custom-call | bytes 25900000 | tf_op jit(solution)/shard_map/widen/pallas_call | solution.py:29
  (258 shorter events, 66.9 us)
Async XLA Ops:
  7.2 25.1 %copy-start = (bf16[1024,512]{1,0:T(8,128)(2,1)S(1)}, bf16[1024,512]{1,0:T(8,128)(2,1)}, u32[]{:S(2)}) copy-start(bf16[1024,512]{1,0:T(8,128)(2,1)} %param.37) | copy-start | bytes 3145732
  16.4 12.3 %copy-start.27 = (bf16[1024,512]{1,0:T(8,128)(2,1)S(1)}, bf16[1024,512]{1,0:T(8,128)(2,1)}, u32[]{:S(2)}) copy-start(bf16[1024,512]{1,0:T(8,128)(2,1)} %wq_own.1) | copy-start | bytes 3145732
  16.4 14.7 %copy-start.62 = (s32[8]{0:T(128)S(1)}, s32[8]{0:T(128)}, u32[]{:S(2)}) copy-start(s32[8]{0:T(128)} %param.23) | copy-start | bytes 100
  16.4 15.9 %copy-start.29 = (bf16[128,1024]{1,0:T(8,128)(2,1)S(1)}, bf16[128,1024]{1,0:T(8,128)(2,1)}, u32[]{:S(2)}) copy-start(bf16[128,1024]{1,0:T(8,128)(2,1)} %param.24) | copy-start | bytes 786436
  16.4 26.4 %all-to-all-start = ((bf16[16,3,64,128]{3,2,1,0:T(8,128)(2,1)}), bf16[16,3,64,128]{3,2,1,0:T(8,128)(2,1)}, u32[]{:S(2)}, u32[]{:S(2)}) async-start(bf16[16,3,64,128]{3,2,1,0:T(8,128)(2,1)} %get-tuple-element.139), calls=%async_computation | async-start | bytes 1572864 | tf_op jit(solution)/shard_map/all_to_all | solution.py:1165
  25.9 39.1 %collective-permute-start.2 = (bf16[256,1024]{1,0:T(8,128)(2,1)}, bf16[256,1024]{1,0:T(8,128)(2,1)}, u32[]{:S(2)}, u32[]{:S(2)}) collective-permute-start(bf16[256,1024]{1,0:T(8,128)(2,1)} %constant_dynamic-slice_fusion.4), channel_id=1, source_target_pairs={{0,1},{1,0},{2,3},{3,2},{4,5},{5,4},{6,7},{7,6},{8,9},{9,8},{10,11... | collective-permute-start | bytes 1572872 | tf_op jit(solution)/shard_map/ppermute | solution.py:245
  28.2 36.8 %collective-permute-start = (bf16[256,1024]{1,0:T(8,128)(2,1)}, bf16[256,1024]{1,0:T(8,128)(2,1)}, u32[]{:S(2)}, u32[]{:S(2)}) collective-permute-start(bf16[256,1024]{1,0:T(8,128)(2,1)} %constant_dynamic-slice_fusion.6), channel_id=1, source_target_pairs={{0,1},{1,0},{2,3},{3,2},{4,5},{5,4},{6,7},{7,6},{8,9},{9,8},{10,11... | collective-permute-start | bytes 1572872 | tf_op jit(solution)/shard_map/ppermute | solution.py:245
  29.6 35.5 %collective-permute-start.1 = (bf16[512,512]{1,0:T(8,128)(2,1)}, bf16[512,512]{1,0:T(8,128)(2,1)}, u32[]{:S(2)}, u32[]{:S(2)}) collective-permute-start(bf16[512,512]{1,0:T(8,128)(2,1)} %constant_dynamic-slice_fusion.5), channel_id=1, source_target_pairs={{0,1},{1,0},{2,3},{3,2},{4,5},{5,4},{6,7},{7,6},{8,9},{9,8},{10,11... | collective-permute-start | bytes 1572872 | tf_op jit(solution)/shard_map/ppermute | solution.py:245
  43.8 2.0 collective-permute-start.3
  65.0 12.2 %copy-start.11 = (bf16[256,1024]{1,0:T(8,128)(2,1)S(1)}, bf16[256,1024]{1,0:T(8,128)(2,1)}, u32[]{:S(2)}) copy-start(bf16[256,1024]{1,0:T(8,128)(2,1)} %x_ref.1) | copy-start | bytes 1572868
  66.6 15.6 %all-to-all-start.1 = ((bf16[16,1,64,128]{3,2,1,0:T(8,128)(2,1)}), bf16[16,1,64,128]{3,2,1,0:T(8,128)(2,1)}, u32[]{:S(2)}, u32[]{:S(2)}) async-start(bf16[16,1,64,128]{3,2,1,0:T(8,128)(2,1)} %bitcast_bitcast_fusion), calls=%async_computation.1 | async-start | bytes 524288 | tf_op jit(solution)/shard_map/all_to_all | solution.py:1162
  72.1 170.4 %reduce-scatter.2.cloned.1.call-start = ((), (), s32[]{:S(2)}) async-start(), calls=%async_computation.5 | async-start | bytes 8912896 | tf_op jit(solution)/shard_map/reduce_scatter | solution.py:1217
  72.3 5.6 %collective-permute-start.4 = (bf16[256,1024]{1,0:T(8,128)(2,1)}, bf16[256,1024]{1,0:T(8,128)(2,1)}, u32[]{:S(2)}, u32[]{:S(2)}) collective-permute-start(bf16[256,1024]{1,0:T(8,128)(2,1)} %collective-permute-done.refs_0_), channel_id=1, source_target_pairs={{0,2},{2,0},{4,6},{6,4},{8,10},{10,8},{12,14},{14,12},{16,18},{18,... | collective-permute-start | bytes 1572872 | tf_op jit(solution)/shard_map/ppermute | solution.py:249
  72.8 5.2 %collective-permute-start.5 = (bf16[512,512]{1,0:T(8,128)(2,1)}, bf16[512,512]{1,0:T(8,128)(2,1)}, u32[]{:S(2)}, u32[]{:S(2)}) collective-permute-start(bf16[512,512]{1,0:T(8,128)(2,1)} %collective-permute-done.1.refs_1_), channel_id=1, source_target_pairs={{0,2},{2,0},{4,6},{6,4},{8,10},{10,8},{12,14},{14,12},{16,18},{18,... | collective-permute-start | bytes 1572872 | tf_op jit(solution)/shard_map/ppermute | solution.py:249
  72.9 5.0 %collective-permute-start.6 = (bf16[256,1024]{1,0:T(8,128)(2,1)}, bf16[256,1024]{1,0:T(8,128)(2,1)}, u32[]{:S(2)}, u32[]{:S(2)}) collective-permute-start(bf16[256,1024]{1,0:T(8,128)(2,1)} %collective-permute-done.2.refs_2_), channel_id=1, source_target_pairs={{0,2},{2,0},{4,6},{6,4},{8,10},{10,8},{12,14},{14,12},{16,18},{18,... | collective-permute-start | bytes 1572872 | tf_op jit(solution)/shard_map/ppermute | solution.py:249
  75.7 9.9 %collective-permute-start.8 = (bf16[2,512,128]{2,1,0:T(8,128)(2,1)}, bf16[2,512,128]{2,1,0:T(8,128)(2,1)}, u32[]{:S(2)}, u32[]{:S(2)}) collective-permute-start(bf16[2,512,128]{2,1,0:T(8,128)(2,1)} %get-tuple-element.359), channel_id=1, source_target_pairs={{0,1},{1,0},{2,3},{3,2},{4,5},{5,4},{6,7},{7,6},{8,9},{9,8},{10,11... | collective-permute-start | bytes 786440 | tf_op jit(solution)/shard_map/ppermute | solution.py:245
  78.0 11.8 %copy-start.18 = (f32[1024]{0:T(1024)S(1)}, f32[1024]{0:T(1024)}, u32[]{:S(2)}) copy-start(f32[1024]{0:T(1024)} %param.28) | copy-start | bytes 12292
  78.0 11.8 %copy-start.19 = (f32[1024]{0:T(1024)S(1)}, f32[1024]{0:T(1024)}, u32[]{:S(2)}) copy-start(f32[1024]{0:T(1024)} %param.30) | copy-start | bytes 12292
  82.2 24.6 %copy-start.6 = (bf16[256,1024]{1,0:T(8,128)(2,1)S(1)}, bf16[256,1024]{1,0:T(8,128)(2,1)}, u32[]{:S(2)}) copy-start(bf16[256,1024]{1,0:T(8,128)(2,1)} %dy_ref.3) | copy-start | bytes 1572868
  83.9 15.4 %copy-start.38 = (bf16[8,1,64,128]{3,2,1,0:T(8,128)(2,1)}, bf16[8,1,64,128]{3,2,1,0:T(8,128)(2,1)S(1)}, u32[]{:S(2)}) copy-start(bf16[8,1,64,128]{3,2,1,0:T(8,128)(2,1)S(1)} %get-tuple-element.361) | copy-start | bytes 393220
  83.9 5.3 %collective-permute-start.7 = (bf16[512,128]{1,0:T(8,128)(2,1)S(1)}, bf16[512,128]{1,0:T(8,128)(2,1)S(1)}, u32[]{:S(2)}, u32[]{:S(2)}) collective-permute-start(bf16[512,128]{1,0:T(8,128)(2,1)S(1)} %bitcast.133), channel_id=1, source_target_pairs={{0,1},{1,0},{2,3},{3,2},{4,5},{5,4},{6,7},{7,6},{8,9},{9,8},{10,11... | collective-permute-start | bytes 393224 | tf_op jit(solution)/shard_map/ppermute | solution.py:245
  85.6 21.2 %copy-start.2 = (bf16[1024,2048]{1,0:T(8,128)(2,1)S(1)}, bf16[1024,2048]{1,0:T(8,128)(2,1)}, u32[]{:S(2)}) copy-start(bf16[1024,2048]{1,0:T(8,128)(2,1)} %wi_ref.1) | copy-start | bytes 12582916
  89.8 16.9 %copy-start.1 = (bf16[2048,1024]{1,0:T(8,128)(2,1)S(1)}, bf16[2048,1024]{1,0:T(8,128)(2,1)}, u32[]{:S(2)}) copy-start(bf16[2048,1024]{1,0:T(8,128)(2,1)} %wo_ref.3) | copy-start | bytes 12582916
  99.3 7.5 %collective-permute-start.9 = (bf16[128,1024]{1,0:T(8,128)(2,1)}, bf16[128,1024]{1,0:T(8,128)(2,1)S(1)}, u32[]{:S(2)}, u32[]{:S(2)}) collective-permute-start(bf16[128,1024]{1,0:T(8,128)(2,1)} %get-tuple-element.159.h_own), channel_id=1, source_target_pairs={{0,1},{1,0},{2,3},{3,2},{4,5},{5,4},{6,7},{7,6},{8,9},{9,8},{10,11... | collective-permute-start | bytes 786440 | tf_op jit(solution)/shard_map/ppermute | solution.py:245
  124.6 6.4 %collective-permute-start.10 = (bf16[128,1024]{1,0:T(8,128)(2,1)S(1)}, bf16[128,1024]{1,0:T(8,128)(2,1)S(1)}, u32[]{:S(2)}, u32[]{:S(2)}) collective-permute-start(bf16[128,1024]{1,0:T(8,128)(2,1)S(1)} %copy-done.25), channel_id=1, source_target_pairs={{0,1},{1,0},{2,3},{3,2},{4,5},{5,4},{6,7},{7,6},{8,9},{9,8},{10,11... | collective-permute-start | bytes 786440 | tf_op jit(solution)/shard_map/ppermute | solution.py:245
  143.6 15.0 %copy-start.43 = (bf16[128,1024]{1,0:T(8,128)(2,1)S(1)}, bf16[128,1024]{1,0:T(8,128)(2,1)}, u32[]{:S(2)}) copy-start(bf16[128,1024]{1,0:T(8,128)(2,1)} %get-tuple-element.185.refs_2_) | copy-start | bytes 786436
  143.6 5.2 %collective-permute-start.11 = (bf16[512,128]{1,0:T(8,128)(2,1)}, bf16[512,128]{1,0:T(8,128)(2,1)S(1)}, u32[]{:S(2)}, u32[]{:S(2)}) collective-permute-start(bf16[512,128]{1,0:T(8,128)(2,1)} %get-tuple-element.174), channel_id=1, source_target_pairs={{0,1},{1,0},{2,3},{3,2},{4,5},{5,4},{6,7},{7,6},{8,9},{9,8},{10,11... | collective-permute-start | bytes 393224 | tf_op jit(solution)/shard_map/ppermute | solution.py:245
  150.5 20.5 %all-to-all-start.2 = ((bf16[16,1,64,128]{3,2,1,0:T(8,128)(2,1)}), bf16[16,1,64,128]{3,2,1,0:T(8,128)(2,1)S(1)}, u32[]{:S(2)}, u32[]{:S(2)}) async-start(bf16[16,1,64,128]{3,2,1,0:T(8,128)(2,1)} %bitcast.36), calls=%async_computation.2 | async-start | bytes 524288 | tf_op jit(solution)/shard_map/all_to_all | solution.py:1234
  156.5 14.6 %collective-permute-start.17 = (bf16[512,128]{1,0:T(8,128)(2,1)}, bf16[512,128]{1,0:T(8,128)(2,1)S(1)}, u32[]{:S(2)}, u32[]{:S(2)}) collective-permute-start(bf16[512,128]{1,0:T(8,128)(2,1)} %get-tuple-element.186), channel_id=1, source_target_pairs={{0,1},{1,0},{2,3},{3,2},{4,5},{5,4},{6,7},{7,6},{8,9},{9,8},{10,11... | collective-permute-start | bytes 393224 | tf_op jit(solution)/shard_map/ppermute | solution.py:245
  157.2 13.9 %collective-permute-start.18 = (bf16[512,128]{1,0:T(8,128)(2,1)}, bf16[512,128]{1,0:T(8,128)(2,1)S(1)}, u32[]{:S(2)}, u32[]{:S(2)}) collective-permute-start(bf16[512,128]{1,0:T(8,128)(2,1)} %get-tuple-element.187), channel_id=1, source_target_pairs={{0,1},{1,0},{2,3},{3,2},{4,5},{5,4},{6,7},{7,6},{8,9},{9,8},{10,11... | collective-permute-start | bytes 393224 | tf_op jit(solution)/shard_map/ppermute | solution.py:245
  158.6 12.6 %collective-permute-start.16 = (bf16[128,1024]{1,0:T(8,128)(2,1)S(1)}, bf16[128,1024]{1,0:T(8,128)(2,1)S(1)}, u32[]{:S(2)}, u32[]{:S(2)}) collective-permute-start(bf16[128,1024]{1,0:T(8,128)(2,1)S(1)} %copy-done.43), channel_id=1, source_target_pairs={{0,1},{1,0},{2,3},{3,2},{4,5},{5,4},{6,7},{7,6},{8,9},{9,8},{10,11... | collective-permute-start | bytes 786440 | tf_op jit(solution)/shard_map/ppermute | solution.py:245
  191.7 2.0 collective-permute-start.19
  194.4 12.1 %copy-start.44 = (bf16[128,1024]{1,0:T(8,128)(2,1)S(1)}, bf16[128,1024]{1,0:T(8,128)(2,1)}, u32[]{:S(2)}) copy-start(bf16[128,1024]{1,0:T(8,128)(2,1)} %get-tuple-element.178.refs_6_) | copy-start | bytes 786436
  198.0 37.1 %all-to-all-start.3 = ((bf16[16,3,64,128]{3,2,1,0:T(8,128)(2,1)}), bf16[16,3,64,128]{3,2,1,0:T(8,128)(2,1)S(1)}, u32[]{:S(2)}, u32[]{:S(2)}) async-start(bf16[16,3,64,128]{3,2,1,0:T(8,128)(2,1)} %combine.1), calls=%async_computation.3 | async-start | bytes 1572864 | tf_op jit(solution)/shard_map/all_to_all | solution.py:1162
  203.7 180.4 %all-gather.4.cloned.1.call-start = ((), (), s32[]{:S(2)}) async-start(), calls=%async_computation.6 | async-start | bytes 8912896 | tf_op jit(solution)/shard_map/all_gather | solution.py:1270
  203.8 9.4 %collective-permute-start.12 = (bf16[2,512,128]{2,1,0:T(8,128)(2,1)}, bf16[2,512,128]{2,1,0:T(8,128)(2,1)S(1)}, u32[]{:S(2)}, u32[]{:S(2)}) collective-permute-start(bf16[2,512,128]{2,1,0:T(8,128)(2,1)} %get-tuple-element.175), channel_id=1, source_target_pairs={{0,1},{1,0},{2,3},{3,2},{4,5},{5,4},{6,7},{7,6},{8,9},{9,8},{10,11... | collective-permute-start | bytes 786440 | tf_op jit(solution)/shard_map/ppermute | solution.py:245
  204.5 14.3 %collective-permute-start.13 = (bf16[128,1024]{1,0:T(8,128)(2,1)S(1)}, bf16[128,1024]{1,0:T(8,128)(2,1)S(1)}, u32[]{:S(2)}, u32[]{:S(2)}) collective-permute-start(bf16[128,1024]{1,0:T(8,128)(2,1)S(1)} %copy-done.42), channel_id=1, source_target_pairs={{0,1},{1,0},{2,3},{3,2},{4,5},{5,4},{6,7},{7,6},{8,9},{9,8},{10,11... | collective-permute-start | bytes 786440 | tf_op jit(solution)/shard_map/ppermute | solution.py:245
  205.9 18.5 %collective-permute-start.14 = (bf16[128,1024]{1,0:T(8,128)(2,1)}, bf16[128,1024]{1,0:T(8,128)(2,1)S(1)}, u32[]{:S(2)}, u32[]{:S(2)}) collective-permute-start(bf16[128,1024]{1,0:T(8,128)(2,1)} %get-tuple-element.177), channel_id=1, source_target_pairs={{0,1},{1,0},{2,3},{3,2},{4,5},{5,4},{6,7},{7,6},{8,9},{9,8},{10,11... | collective-permute-start | bytes 786440 | tf_op jit(solution)/shard_map/ppermute | solution.py:245
  206.5 23.0 %collective-permute-start.15 = (bf16[128,1024]{1,0:T(8,128)(2,1)S(1)}, bf16[128,1024]{1,0:T(8,128)(2,1)S(1)}, u32[]{:S(2)}, u32[]{:S(2)}) collective-permute-start(bf16[128,1024]{1,0:T(8,128)(2,1)S(1)} %copy-done.44), channel_id=1, source_target_pairs={{0,1},{1,0},{2,3},{3,2},{4,5},{5,4},{6,7},{7,6},{8,9},{9,8},{10,11... | collective-permute-start | bytes 786440 | tf_op jit(solution)/shard_map/ppermute | solution.py:245
  242.6 190.1 %all-gather.6.cloned.1.call-start = ((), (), s32[]{:S(2)}) async-start(), calls=%async_computation.7 | async-start | bytes 6684672 | tf_op jit(solution)/shard_map/all_gather | solution.py:1295
  242.9 16.5 %collective-permute-start.20 = (bf16[256,3072]{1,0:T(8,128)(2,1)}, bf16[256,3072]{1,0:T(8,128)(2,1)}, u32[]{:S(2)}, u32[]{:S(2)}) collective-permute-start(bf16[256,3072]{1,0:T(8,128)(2,1)} %get-tuple-element.200), channel_id=1, source_target_pairs={{0,2},{2,0},{4,6},{6,4},{8,10},{10,8},{12,14},{14,12},{16,18},{18,... | collective-permute-start | bytes 4718600 | tf_op jit(solution)/shard_map/ppermute | solution.py:249
  243.1 16.3 %collective-permute-start.21 = (bf16[512,1536]{1,0:T(8,128)(2,1)}, bf16[512,1536]{1,0:T(8,128)(2,1)}, u32[]{:S(2)}, u32[]{:S(2)}) collective-permute-start(bf16[512,1536]{1,0:T(8,128)(2,1)} %get-tuple-element.205), channel_id=1, source_target_pairs={{0,2},{2,0},{4,6},{6,4},{8,10},{10,8},{12,14},{14,12},{16,18},{18,... | collective-permute-start | bytes 4718600 | tf_op jit(solution)/shard_map/ppermute | solution.py:249
  243.7 7.5 %collective-permute-start.22 = (bf16[2,512,128]{2,1,0:T(8,128)(2,1)S(1)}, bf16[2,512,128]{2,1,0:T(8,128)(2,1)S(1)}, u32[]{:S(2)}, u32[]{:S(2)}) collective-permute-start(bf16[2,512,128]{2,1,0:T(8,128)(2,1)S(1)} %fusion.15), channel_id=1, source_target_pairs={{0,2},{2,0},{4,6},{6,4},{8,10},{10,8},{12,14},{14,12},{16,18},{18,... | collective-permute-start | bytes 786440 | tf_op jit(solution)/shard_map/ppermute | solution.py:249
  245.1 9.2 %collective-permute-start.24 = (bf16[128,1024]{1,0:T(8,128)(2,1)S(1)}, bf16[128,1024]{1,0:T(8,128)(2,1)S(1)}, u32[]{:S(2)}, u32[]{:S(2)}) collective-permute-start(bf16[128,1024]{1,0:T(8,128)(2,1)S(1)} %add_convert_fusion.1), channel_id=1, source_target_pairs={{0,1},{1,0},{2,3},{3,2},{4,5},{5,4},{6,7},{7,6},{8,9},{9,8},{10,11... | collective-permute-start | bytes 786440 | tf_op jit(solution)/shard_map/ppermute | solution.py:245
  249.8 9.6 %collective-permute-start.23 = (bf16[128,1024]{1,0:T(8,128)(2,1)}, bf16[128,1024]{1,0:T(8,128)(2,1)S(1)}, u32[]{:S(2)}, u32[]{:S(2)}) collective-permute-start(bf16[128,1024]{1,0:T(8,128)(2,1)} %get-tuple-element.208), channel_id=1, source_target_pairs={{0,1},{1,0},{2,3},{3,2},{4,5},{5,4},{6,7},{7,6},{8,9},{9,8},{10,11... | collective-permute-start | bytes 786440 | tf_op jit(solution)/shard_map/ppermute | solution.py:245
  265.6 34.3 %collective-permute-start.25 = (bf16[128,3072]{1,0:T(8,128)(2,1)}, bf16[128,3072]{1,0:T(8,128)(2,1)S(1)}, u32[]{:S(2)}, u32[]{:S(2)}) collective-permute-start(bf16[128,3072]{1,0:T(8,128)(2,1)} %get-tuple-element.217), channel_id=1, source_target_pairs={{0,4},{2,6},{4,0},{6,2},{8,12},{10,14},{12,8},{14,10},{16,20},{18,... | collective-permute-start | bytes 2359304 | tf_op jit(solution)/shard_map/ppermute | solution.py:249
  267.2 33.9 %collective-permute-start.26 = (bf16[256,1536]{1,0:T(8,128)(2,1)}, bf16[256,1536]{1,0:T(8,128)(2,1)S(1)}, u32[]{:S(2)}, u32[]{:S(2)}) collective-permute-start(bf16[256,1536]{1,0:T(8,128)(2,1)} %get-tuple-element.218), channel_id=1, source_target_pairs={{0,8},{2,10},{4,12},{6,14},{8,0},{10,2},{12,4},{14,6},{16,24},{18,... | collective-permute-start | bytes 2359304 | tf_op jit(solution)/shard_map/ppermute | solution.py:249
  268.3 7.9 %collective-permute-start.28 = (bf16[128,1024]{1,0:T(8,128)(2,1)S(1)}, bf16[128,1024]{1,0:T(8,128)(2,1)S(1)}, u32[]{:S(2)}, u32[]{:S(2)}) collective-permute-start(bf16[128,1024]{1,0:T(8,128)(2,1)S(1)} %fusion.12), channel_id=1, source_target_pairs={{0,1},{1,0},{2,3},{3,2},{4,5},{5,4},{6,7},{7,6},{8,9},{9,8},{10,11... | collective-permute-start | bytes 786440 | tf_op jit(solution)/shard_map/ppermute | solution.py:245
  269.4 30.5 %collective-permute-start.27 = (bf16[2,512,128]{2,1,0:T(8,128)(2,1)S(1)}, bf16[2,512,128]{2,1,0:T(8,128)(2,1)S(1)}, u32[]{:S(2)}, u32[]{:S(2)}) collective-permute-start(bf16[2,512,128]{2,1,0:T(8,128)(2,1)S(1)} %get-tuple-element.345), channel_id=1, source_target_pairs={{0,4},{2,6},{4,0},{6,2},{8,12},{10,14},{12,8},{14,10},{16,20},{18,... | collective-permute-start | bytes 786440 | tf_op jit(solution)/shard_map/ppermute | solution.py:249
  269.5 6.7 %collective-permute-start.29 = (f32[6,1024]{1,0:T(8,128)S(1)}, f32[6,1024]{1,0:T(8,128)S(1)}, u32[]{:S(2)}, u32[]{:S(2)}) collective-permute-start(f32[6,1024]{1,0:T(8,128)S(1)} %pad_maximum_fusion.5), channel_id=1, source_target_pairs={{0,1},{1,0},{2,3},{3,2},{4,5},{5,4},{6,7},{7,6},{8,9},{9,8},{10,11... | collective-permute-start | bytes 73736 | tf_op jit(solution)/shard_map/ppermute | solution.py:245
  276.2 35.0 %copy-start.50 = (bf16[128,1024]{1,0:T(8,128)(2,1)}, bf16[128,1024]{1,0:T(8,128)(2,1)S(1)}, u32[]{:S(2)}) copy-start(bf16[128,1024]{1,0:T(8,128)(2,1)S(1)} %collective-permute-done.28) | copy-start | bytes 786436
  306.9 29.0 %collective-permute-start.30 = (bf16[64,3072]{1,0:T(8,128)(2,1)}, bf16[64,3072]{1,0:T(8,128)(2,1)S(1)}, u32[]{:S(2)}, u32[]{:S(2)}) collective-permute-start(bf16[64,3072]{1,0:T(8,128)(2,1)} %get-tuple-element.227), channel_id=1, source_target_pairs={{0,8},{2,10},{4,12},{6,14},{8,0},{10,2},{12,4},{14,6},{16,24},{18,... | collective-permute-start | bytes 1179656 | tf_op jit(solution)/shard_map/ppermute | solution.py:249
  306.9 29.0 %collective-permute-start.31 = (bf16[128,1536]{1,0:T(8,128)(2,1)}, bf16[128,1536]{1,0:T(8,128)(2,1)S(1)}, u32[]{:S(2)}, u32[]{:S(2)}) collective-permute-start(bf16[128,1536]{1,0:T(8,128)(2,1)} %get-tuple-element.228), channel_id=1, source_target_pairs={{0,4},{2,6},{4,0},{6,2},{8,12},{10,14},{12,8},{14,10},{16,20},{18,... | collective-permute-start | bytes 1179656 | tf_op jit(solution)/shard_map/ppermute | solution.py:249
  309.3 26.6 %collective-permute-start.32 = (bf16[2,512,128]{2,1,0:T(8,128)(2,1)}, bf16[2,512,128]{2,1,0:T(8,128)(2,1)S(1)}, u32[]{:S(2)}, u32[]{:S(2)}) collective-permute-start(bf16[2,512,128]{2,1,0:T(8,128)(2,1)} %fusion.16), channel_id=1, source_target_pairs={{0,8},{2,10},{4,12},{6,14},{8,0},{10,2},{12,4},{14,6},{16,24},{18,... | collective-permute-start | bytes 786440 | tf_op jit(solution)/shard_map/ppermute | solution.py:249
  311.3 1.3 collective-permute-start.33
  336.1 30.9 %collective-permute-start.36 = (bf16[2,512,128]{2,1,0:T(8,128)(2,1)S(1)}, bf16[2,512,128]{2,1,0:T(8,128)(2,1)S(1)}, u32[]{:S(2)}, u32[]{:S(2)}) collective-permute-start(bf16[2,512,128]{2,1,0:T(8,128)(2,1)S(1)} %fusion.20), channel_id=1, source_target_pairs={{0,16},{2,18},{4,20},{6,22},{8,24},{10,26},{12,28},{14,30},{16,0},... | collective-permute-start | bytes 786440 | tf_op jit(solution)/shard_map/ppermute | solution.py:249
  342.2 29.5 %copy-start.51 = (bf16[128,1024]{1,0:T(8,128)(2,1)S(1)}, bf16[128,1024]{1,0:T(8,128)(2,1)}, u32[]{:S(2)}) copy-start(bf16[128,1024]{1,0:T(8,128)(2,1)} %copy-done.50) | copy-start | bytes 786436
  342.2 22.3 %collective-permute-start.34 = (bf16[32,3072]{1,0:T(8,128)(2,1)}, bf16[32,3072]{1,0:T(8,128)(2,1)S(1)}, u32[]{:S(2)}, u32[]{:S(2)}) collective-permute-start(bf16[32,3072]{1,0:T(8,128)(2,1)} %get-tuple-element.235), channel_id=1, source_target_pairs={{0,16},{2,18},{4,20},{6,22},{8,24},{10,26},{12,28},{14,30},{16,0},... | collective-permute-start | bytes 589832 | tf_op jit(solution)/shard_map/ppermute | solution.py:249
  343.4 23.5 %collective-permute-start.35 = (bf16[64,1536]{1,0:T(8,128)(2,1)}, bf16[64,1536]{1,0:T(8,128)(2,1)S(1)}, u32[]{:S(2)}, u32[]{:S(2)}) collective-permute-start(bf16[64,1536]{1,0:T(8,128)(2,1)} %get-tuple-element.236), channel_id=1, source_target_pairs={{0,16},{2,18},{4,20},{6,22},{8,24},{10,26},{12,28},{14,30},{16,0},... | collective-permute-start | bytes 589832 | tf_op jit(solution)/shard_map/ppermute | solution.py:249
  345.2 3.9 collective-permute-start.37
  372.6 4.2 collective-permute-start.39
  375.2 8.0 %collective-permute-start.38 = (bf16[128,1024]{1,0:T(8,128)(2,1)S(1)}, bf16[128,1024]{1,0:T(8,128)(2,1)S(1)}, u32[]{:S(2)}, u32[]{:S(2)}) collective-permute-start(bf16[128,1024]{1,0:T(8,128)(2,1)S(1)} %fusion), channel_id=1, source_target_pairs={{0,1},{1,0},{2,3},{3,2},{4,5},{5,4},{6,7},{7,6},{8,9},{9,8},{10,11... | collective-permute-start | bytes 786440 | tf_op jit(solution)/shard_map/ppermute | solution.py:245
  376.8 5.3 %collective-permute-start.40 = (f32[6,1024]{1,0:T(8,128)S(1)}, f32[6,1024]{1,0:T(8,128)S(1)}, u32[]{:S(2)}, u32[]{:S(2)}) collective-permute-start(f32[6,1024]{1,0:T(8,128)S(1)} %add.321), channel_id=1, source_target_pairs={{0,16},{2,18},{4,20},{6,22},{8,24},{10,26},{12,28},{14,30},{16,0},... | collective-permute-start | bytes 73736 | tf_op jit(solution)/shard_map/ppermute | solution.py:249
  388.8 43.9 %copy-start.23 = (s32[2,16]{1,0:T(2,128)S(1)}, s32[2,16]{1,0:T(2,128)}, u32[]{:S(2)}) copy-start(s32[2,16]{1,0:T(2,128)} %constant.159.clone.devices) | copy-start | bytes 388
  (47 other events, 192.2 us)
Sparse Core Ops, SparseCore 0:
  123.8 118.7 reduce-scatter.1
  244.7 90.9 all-gather.3
  369.9 62.7 all-gather.5
